TPU v7x, 256 devices: a whole 4x4x8 slice. The times are simulated.
256 devices in a mesh: ens: 16 (over x_hi, z), lon: 4 (over x_lo, core), lat: 4 (over y).
Axes of the slice: x: 4 (x_hi: 2, x_lo: 2; x = x_hi * 2 + x_lo), y: 4, z: 8, core: 2. Of those that a mesh axis runs over, the one named last changes fastest.
Arguments:
- members: float32 [16, 80, 32, 640], P('ens', 'lat', 'lon'), may hold values from -6 to 6
- analysis: float32 [80, 32, 640], P('lat', 'lon', 'ens'), may hold values from -6 to 6
- stencils: float32 [7, 7, 7, 80], replicated, may hold values from -0.84 to 0.84
- mixing: float32 [7, 640, 640], replicated, may hold values from -0.09375 to 0.09375
Outputs:
- members_grad: float32 [16, 80, 32, 640], P('ens', 'lat', 'lon')
- crps_field: float32 [80, 32, 640], P('lat', 'lon', 'ens')
All inputs are finite; a program needn't handle non-finite values.
Results may differ from a plain program's by a relative error of at most 0.00016.
Values sent between devices are 32-bit elements; how exact they have to be, the bound alone decides.
A program may use at most 128 MiB of HBM per device.

v0:
```python
import jax
import jax.numpy as jnp
from jax import lax
from jax.sharding import PartitionSpec as P

BASES = 7
SPAN = 7


smooth = 0.01
highest = lax.Precision.HIGHEST


def extended_2(block, sides, width, periodic):
    for axis, dim in sides:
        count = lax.axis_size(axis)
        forward = [(i, i + 1) for i in range(count - 1)]
        if periodic:
            forward.append((count - 1, 0))
        backward = [(target, source) for source, target in forward]
        low = lax.ppermute(
            lax.slice_in_dim(block, block.shape[dim] - width, None, axis=dim), axis, forward
        )
        high = lax.ppermute(lax.slice_in_dim(block, 0, width, axis=dim), axis, backward)
        block = jnp.concatenate([low, block, high], axis=dim)
    return block


def extend(field_block):
    margin = SPAN // 2
    widened = extended_2(field_block, (("lon", 2),), margin, True)
    return extended_2(widened, (("lat", 1),), margin, False)


def apply_taps(extended, weights, height, breadth):
    running = jnp.zeros(
        (weights.shape[0], extended.shape[0], height, breadth, extended.shape[3]), jnp.float32
    )
    for row_tap in range(SPAN):
        for col_tap in range(SPAN):
            tap_index = row_tap * SPAN + col_tap
            running = (
                running
                + weights[:, tap_index, None, :, None, None]
                * extended[None, :, row_tap : row_tap + height, col_tap : col_tap + breadth, :]
            )
    return jnp.transpose(running, (1, 2, 3, 0, 4))


def local(members, analysis, stencils, mixing):
    own_count, height, breadth, channels = members.shape
    margin = SPAN // 2
    first_row = lax.axis_index("lat") * height
    padded = jnp.pad(stencils, ((0, 0), (0, 0), (0, 0), (margin, margin)))
    window = lax.dynamic_slice_in_dim(padded, first_row, height + 2 * margin, 3)
    forward = window[:, :, :, margin : margin + height].reshape(BASES, SPAN * SPAN, height)
    backward = jnp.stack(
        [
            window[:, SPAN - 1 - row_tap, ::-1, row_tap : row_tap + height]
            for row_tap in range(SPAN)
        ],
        axis=1,
    ).reshape(BASES, SPAN * SPAN, height)
    stencilled = apply_taps(extend(members), forward, height, breadth)
    mixed = jnp.dot(
        stencilled.reshape(-1, BASES * channels),
        mixing.reshape(BASES * channels, channels),
        precision=highest,
        preferred_element_type=jnp.float32,
    )
    bounded_activation = jnp.tanh(mixed.reshape(own_count, height, breadth, channels))
    predicted_fields = members + bounded_activation
    observed_truth = lax.all_gather(analysis, "ens", axis=2, tiled=True)
    prediction_error = predicted_fields - observed_truth[None]
    differ = (
        prediction_error[:, None]
        - lax.all_gather(prediction_error, "ens", axis=0, tiled=True)[None]
    )
    smooth_abs = jnp.sqrt(differ * differ + smooth)
    sum_abs = jnp.sum(smooth_abs, 1)
    sum_slope = jnp.sum(differ / smooth_abs, 1)
    members_total = own_count * lax.axis_size("ens")
    own_abs = jnp.sqrt(prediction_error * prediction_error + smooth)
    partial_score_sums = jnp.sum(
        own_abs / members_total - sum_abs / (2.0 * members_total * (members_total - 1)), 0
    )
    crps_field = lax.psum_scatter(partial_score_sums, "ens", scatter_dimension=2, tiled=True)
    grad_out = prediction_error / own_abs - sum_slope / (members_total - 1.0)
    inner_grad = grad_out * (1.0 - bounded_activation * bounded_activation)
    spread = apply_taps(extend(inner_grad), backward, height, breadth)
    adjoint = lax.dot_general(
        spread.reshape(-1, BASES, channels),
        mixing,
        (((1, 2), (0, 2)), ((), ())),
        precision=highest,
        preferred_element_type=jnp.float32,
    )
    members_grad = grad_out + adjoint.reshape(own_count, height, breadth, channels)
    return (members_grad, crps_field)


def solution(mesh):
    in_specs = (P("ens", "lat", "lon", None), P("lat", "lon", "ens"), P(), P())
    out_specs = (P("ens", "lat", "lon", None), P("lat", "lon", "ens"))
    return jax.shard_map(local, mesh=mesh, in_specs=in_specs, out_specs=out_specs, check_vma=False)
```

profile of v0, /device:TPU:1, one launch (start us, length us, event | category | flops | bytes accessed | tf_op | source)
XLA Modules:
  0.0 505.5 jit_solution(6073563373159299852)
XLA Ops:
  7.2 2.0 fusion.228
  9.2 2.6 collective-permute-start
  13.6 1.7 copy.254
  43.6 53.7 %all_gather.6 = f32[20,8,640]{0,1,2:T(8,128)S(1)} all-gather(f32[20,8,40]{0,1,2:T(8,128)} %copy.254), channel_id=1, replica_groups=mesh['ens'=16,'lon'=4,'lat'=4] {'ens'}, dimensions={2}, use_global_device_ids=true | all-gather | bytes 435200 | tf_op jit(solution)/shard_map/all_gather | solution.py:73
  97.3 1.7 copy.255
  99.0 3.2 collective-permute-start.2
  104.1 3.8 collective-permute-done.3
  108.0 1.5 slice_bitcast_fusion.86
  110.0 3.3 slice_bitcast_fusion.62
  113.7 18.8 %multiply_add_fusion = f32[7,1,20,8,640]{4,3,0,2,1:T(8,128)S(1)} fusion(f32[20,8,640]{2,1,0:T(8,128)} %get-tuple-element.68, f32[7,20]{0,1:T(8,128)S(1)} %copy-done.36, f32[20,8,640]{2,1,0:T(8,128)} %get-tuple-element.69, f32[7,20]{0,1:T(8,128)S(1)} %copy-done.37, f32[20,8,640]{2,1,0:T(8,128)} %get-tuple-element.70, f32[7,20]{0,1:T(8,128)S(1)} %copy-done.38, ...), kind=kLoop, calls=%fused_computation.104 | loop fusion | flops 69529600 | bytes 22965040 | tf_op jit(solution)/shard_map/add | solution.py:43
  132.6 8.8 %bitcast_subtract_fusion.2 = (f32[1,20,8,640]{3,2,1,0:T(8,128)}, f32[20,8,640]{2,1,0:T(8,128)S(1)}) fusion(f32[20,8,640]{2,1,0:T(8,128)S(1)} %copy-done.3, f32[1,20,8,640]{3,2,1,0:T(8,128)S(1)} %copy-done, f32[20,8,4480]{2,1,0:T(8,128)S(1)} %bitcast.460, f32[4480,640,1]{1,0,2:T(8,128)S(1)} %bitcast.457), kind=kOutput, calls=%fused_computation.331 | convolution fusion | flops 5505228800 | bytes 15974400 | tf_op jit(solution)/shard_map/dot_general | solution.py:65
  143.3 119.7 %all-gather.2.cloned.1.call-done = f32[16,20,8,640]{3,2,1,0:T(8,128)} async-done(((f32[1,20,8,640]{3,2,1,0:T(8,128)}), f32[16,20,8,640]{3,2,1,0:T(8,128)}) %all-gather.2.cloned.1.call-update) | async-done | bytes 6553616 | tf_op jit(solution)/shard_map/all_gather | solution.py:77
  263.0 6.4 %fusion.2 = (f32[20,8,640]{2,1,0:T(8,128)S(1)}, f32[20,8,640]{2,1,0:T(8,128)S(1)}) fusion(f32[16,20,8,640]{3,2,1,0:T(8,128)} %all-gather.2.cloned.1.call-done, f32[20,8,640]{2,1,0:T(8,128)S(1)} %bitcast.461), kind=kLoop, calls=%fused_computation.3 | loop fusion | flops 9625600 | bytes 7782400 | tf_op jit(solution)/shard_map/reduce_sum | solution.py:80
  269.8 1.4 collective-permute-start.4
  290.8 4.9 copy.307
  295.7 5.6 %reshape.1431 = f32[640,160]{1,0:T(8,128)} reshape(f32[640,20,8]{2,1,0:T(8,128)} %bitcast.452) | data formatting | bytes 819200
  301.4 3.1 collective-permute-start.6
  304.5 1.3 collective-permute-start.7
  306.4 3.8 collective-permute-done.7
  310.4 3.2 slice_bitcast_fusion.20
  314.5 3.9 slice_bitcast_fusion.41
  318.5 20.4 %fusion.234 = f32[20,8,7,640]{3,1,2,0:T(8,128)S(1)} fusion(f32[20,8,640]{2,1,0:T(8,128)} %get-tuple-element.26, f32[7,20]{0,1:T(8,128)} %copy.305, f32[20,8,640]{2,1,0:T(8,128)} %get-tuple-element.27, f32[7,20]{0,1:T(8,128)} %copy.304, f32[20,8,640]{2,1,0:T(8,128)} %get-tuple-element.28, f32[7,20]{0,1:T(8,128)} %copy.303, ...), kind=kLoop, calls=%fused_computation.6.clone.clone.clone.clone.clone.1 | loop fusion | flops 69529600 | bytes 22965040 | tf_op jit(solution)/shard_map/dot_general | solution.py:91
  339.0 12.2 %fusion.206 = f32[1,20,8,640]{3,2,1,0:T(8,128)} fusion(f32[7,640,640]{2,1,0:T(8,128)S(1)} %bitcast.459, f32[20,8,640]{2,1,0:T(8,128)S(1)} %copy-done.7, f32[1,20,8,640]{3,2,1,0:T(8,128)S(1)} %copy-done.1, f32[20,8,7,640]{3,1,2,0:T(8,128)S(1)} %fusion.234), kind=kOutput, calls=%fused_computation.205 | convolution fusion | flops 5505638400 | bytes 15564800 | tf_op jit(solution)/shard_map/dot_general | solution.py:91
  351.1 145.5 %reduce-scatter.4.cloned.1.call-done = f32[40,160]{1,0:T(8,128)} async-done(((f32[640,160]{1,0:T(8,128)}), f32[40,160]{1,0:T(8,128)}) %reduce-scatter.4.cloned.1.call-update) | async-done | bytes 25616
  (261 shorter events, 57.7 us)
Async XLA Ops:
  7.2 255.9 %all-gather.2.cloned.1.call-start = ((), (), s32[]{:S(2)}) async-start(), calls=%async_computation.1 | async-start | bytes 6963200 | tf_op jit(solution)/shard_map/all_gather | solution.py:77
  9.2 89.8 %collective-permute-start = (f32[1,20,3,640]{3,2,1,0:T(4,128)}, f32[1,20,3,640]{3,2,1,0:T(4,128)S(1)}, u32[]{:S(2)}, u32[]{:S(2)}) collective-permute-start(f32[1,20,3,640]{3,2,1,0:T(4,128)} %get-tuple-element.116), channel_id=1, source_target_pairs={{0,4},{4,8},{8,12},{12,0},{1,5},{5,9},{9,13},{13,1},{2,6},{6,10},{... | collective-permute-start | bytes 460808 | tf_op jit(solution)/shard_map/ppermute | solution.py:21
  11.8 87.2 %collective-permute-start.1 = (f32[1,20,3,640]{3,2,1,0:T(4,128)}, f32[1,20,3,640]{3,2,1,0:T(4,128)S(1)}, u32[]{:S(2)}, u32[]{:S(2)}) collective-permute-start(f32[1,20,3,640]{3,2,1,0:T(4,128)} %get-tuple-element.117), channel_id=1, source_target_pairs={{4,0},{8,4},{12,8},{0,12},{5,1},{9,5},{13,9},{1,13},{6,2},{10,6},{... | collective-permute-start | bytes 460808 | tf_op jit(solution)/shard_map/ppermute | solution.py:24
  43.6 55.4 %copy-start = (f32[1,20,8,640]{3,2,1,0:T(8,128)S(1)}, f32[1,20,8,640]{3,2,1,0:T(8,128)}, u32[]{:S(2)}) copy-start(f32[1,20,8,640]{3,2,1,0:T(8,128)} %param.4) | copy-start | bytes 1228804
  99.0 5.1 %collective-permute-start.2 = (f32[1,3,14,640]{3,2,1,0:T(8,128)S(1)}, f32[1,3,14,640]{3,2,1,0:T(8,128)S(1)}, u32[]{:S(2)}, u32[]{:S(2)}) collective-permute-start(f32[1,3,14,640]{3,2,1,0:T(8,128)S(1)} %get-tuple-element.94), channel_id=1, source_target_pairs={{0,1},{1,2},{2,3},{4,5},{5,6},{6,7},{8,9},{9,10},{10,11},{12,13},{... | collective-permute-start | bytes 322568 | tf_op jit(solution)/shard_map/ppermute | solution.py:21
  102.2 5.6 %collective-permute-start.3 = (f32[1,3,14,640]{3,2,1,0:T(8,128)S(1)}, f32[1,3,14,640]{3,2,1,0:T(8,128)S(1)}, u32[]{:S(2)}, u32[]{:S(2)}) collective-permute-start(f32[1,3,14,640]{3,2,1,0:T(8,128)S(1)} %get-tuple-element.95), channel_id=1, source_target_pairs={{1,0},{2,1},{3,2},{5,4},{6,5},{7,6},{9,8},{10,9},{11,10},{13,12},{... | collective-permute-start | bytes 322568 | tf_op jit(solution)/shard_map/ppermute | solution.py:24
  113.3 19.2 %slice-start = ((s8[11468800]{0:T(1024)(128)(4,1)}), s8[4194304]{0:T(1024)(128)(4,1)S(1)}, s32[]{:S(2)}) async-start(s8[11468800]{0:T(1024)(128)(4,1)} %bitcast.455), calls=%async_computation.3 | async-start | bytes 8388608
  113.7 18.9 %slice-start.1 = ((s8[11468800]{0:T(1024)(128)(4,1)}), s8[4194304]{0:T(1024)(128)(4,1)S(1)}, s32[]{:S(2)}) async-start(s8[11468800]{0:T(1024)(128)(4,1)} %bitcast.455), calls=%async_computation.4 | async-start | bytes 8388608
  113.7 18.9 %slice-start.2 = ((s8[11468800]{0:T(1024)(128)(4,1)}), s8[3080192]{0:T(1024)(128)(4,1)S(1)}, s32[]{:S(2)}) async-start(s8[11468800]{0:T(1024)(128)(4,1)} %bitcast.455), calls=%async_computation.5 | async-start | bytes 6160384
  113.7 18.9 %copy-start.3 = (f32[20,8,640]{2,1,0:T(8,128)S(1)}, f32[20,8,640]{2,1,0:T(8,128)}, u32[]{:S(2)}) copy-start(f32[20,8,640]{2,1,0:T(8,128)} %copy.255) | copy-start | bytes 1228804
  132.5 9.1 %copy-start.2 = (f32[7,7,7,80]{3,2,1,0:T(8,128)S(1)}, f32[7,7,7,80]{3,2,1,0:T(8,128)}, u32[]{:S(2)}) copy-start(f32[7,7,7,80]{3,2,1,0:T(8,128)} %param.6) | copy-start | bytes 329284
  141.4 121.7 %copy-start.1 = (f32[1,20,8,640]{3,2,1,0:T(8,128)S(1)}, f32[1,20,8,640]{3,2,1,0:T(8,128)}, u32[]{:S(2)}) copy-start(f32[1,20,8,640]{3,2,1,0:T(8,128)} %get-tuple-element.222) | copy-start | bytes 1228804
  141.4 355.3 %reduce-scatter.4.cloned.1.call-start = ((), (), s32[]{:S(2)}) async-start(), calls=%async_computation.2 | async-start | bytes 696320
  269.8 31.5 %collective-permute-start.4 = (f32[1,20,3,640]{3,2,1,0:T(4,128)S(1)}, f32[1,20,3,640]{3,2,1,0:T(4,128)S(1)}, u32[]{:S(2)}, u32[]{:S(2)}) collective-permute-start(f32[1,20,3,640]{3,2,1,0:T(4,128)S(1)} %get-tuple-element.113), channel_id=1, source_target_pairs={{0,4},{4,8},{8,12},{12,0},{1,5},{5,9},{9,13},{13,1},{2,6},{6,10},{... | collective-permute-start | bytes 460808 | tf_op jit(solution)/shard_map/ppermute | solution.py:21
  271.2 30.1 %collective-permute-start.5 = (f32[1,20,3,640]{3,2,1,0:T(4,128)S(1)}, f32[1,20,3,640]{3,2,1,0:T(4,128)S(1)}, u32[]{:S(2)}, u32[]{:S(2)}) collective-permute-start(f32[1,20,3,640]{3,2,1,0:T(4,128)S(1)} %get-tuple-element.114), channel_id=1, source_target_pairs={{4,0},{8,4},{12,8},{0,12},{5,1},{9,5},{13,9},{1,13},{6,2},{10,6},{... | collective-permute-start | bytes 460808 | tf_op jit(solution)/shard_map/ppermute | solution.py:24
  301.4 5.0 collective-permute-start.6
  304.5 5.6 %collective-permute-start.7 = (f32[1,3,14,640]{3,2,1,0:T(8,128)S(1)}, f32[1,3,14,640]{3,2,1,0:T(8,128)S(1)}, u32[]{:S(2)}, u32[]{:S(2)}) collective-permute-start(f32[1,3,14,640]{3,2,1,0:T(8,128)S(1)} %get-tuple-element.91), channel_id=1, source_target_pairs={{1,0},{2,1},{3,2},{5,4},{6,5},{7,6},{9,8},{10,9},{11,10},{13,12},{... | collective-permute-start | bytes 322568 | tf_op jit(solution)/shard_map/ppermute | solution.py:24
  314.4 4.0 copy-start.22
  314.4 4.0 copy-start.24
  314.5 4.0 copy-start.26
  314.5 24.5 %slice-start.3 = ((s8[11468800]{0:T(1024)(128)(4,1)}), s8[3080192]{0:T(1024)(128)(4,1)S(1)}, s32[]{:S(2)}) async-start(s8[11468800]{0:T(1024)(128)(4,1)} %bitcast.458), calls=%async_computation.6 | async-start | bytes 6160384
  314.5 24.5 %slice-start.4 = ((s8[11468800]{0:T(1024)(128)(4,1)}), s8[4194304]{0:T(1024)(128)(4,1)S(1)}, s32[]{:S(2)}) async-start(s8[11468800]{0:T(1024)(128)(4,1)} %bitcast.458), calls=%async_computation.7 | async-start | bytes 8388608
  318.5 20.5 %slice-start.5 = ((s8[11468800]{0:T(1024)(128)(4,1)}), s8[4194304]{0:T(1024)(128)(4,1)S(1)}, s32[]{:S(2)}) async-start(s8[11468800]{0:T(1024)(128)(4,1)} %bitcast.458), calls=%async_computation.8 | async-start | bytes 8388608
  318.5 20.5 %copy-start.7 = (f32[20,8,640]{2,1,0:T(8,128)S(1)}, f32[20,8,640]{2,1,0:T(8,128)}, u32[]{:S(2)}) copy-start(f32[20,8,640]{2,1,0:T(8,128)} %copy-done.6) | copy-start | bytes 1228804
  (40 other events, 144.5 us)
Sparse Core Ops, SparseCore 0:
  141.5 121.4 all-gather.1
  301.4 195.1 reduce-scatter.3
where the time goes:
time: 515 us; the launch traced here: 505 us
  waiting for transfers between devices  273 us (53%)
  local copies, waits for them, and re-layouts  81.4 us (16%)
  blocking collectives  53.7 us (10%)
  other arithmetic  46.9 us (9%)
  matrix products  21 us (4%)
  between operations  15.4 us (3%)
  starting transfers between devices  13.9 us (3%)
    unnamed x3, waiting for transfers between devices  146 us
    all_gather x1, waiting for transfers between devices, local(): lax.all_gather(prediction_error, 'ens', axis=0, tiled=True)[None]  120 us
    mul x112, local copies, waits for them, and re-layouts, apply_taps(): weights[:, tap_index, None, :, None, None]  62 us
    all_gather x1, blocking collectives, local(): observed_truth = lax.all_gather(analysis, 'ens', axis=2, tiled=True)  53.7 us
    dot_general x1, other arithmetic, local(): lax.dot_general(spread.reshape(-1, BASES, channels), mixing, (((1, 2), (0...  20.4 us
    add x1, other arithmetic, apply_taps(): running + weights[:, tap_index, None, :, None, None] * extended[None, :,...  18.8 us
    unnamed x119, local copies, waits for them, and re-layouts  14.2 us
    dot_general x1, matrix products, local(): lax.dot_general(spread.reshape(-1, BASES, channels), mixing, (((1, 2), (0...  12.2 us
  transfers between devices with their start and end apart: 10, of which 6 were waited for; matrix products, arithmetic and copies ran while one was open for 21% of the time, Pallas kernels for 0%

commit v1 on v0

v1 whole, which is shorter than its diff:
```python
import functools

import jax
import jax.numpy as jnp
import numpy as np
from jax import lax
from jax.experimental import pallas as pl
from jax.experimental.pallas import tpu as pltpu
from jax.sharding import PartitionSpec as P

BASES = 7
SPAN = 7
MARGIN = 3
ROWS = 20
COLS = 8
WINDOWS = ROWS // 2
EXT = ROWS + 2 * MARGIN
SMOOTH = 0.01
MESH = pl.DeviceIdType.MESH
f32 = jnp.float32
bf16 = jnp.bfloat16


def split(x):
    hi = x.astype(bf16)
    return hi, (x - hi.astype(f32)).astype(bf16)


def mm(a, b):
    return jnp.dot(a, b, preferred_element_type=f32)


def prep_kernel(st_ref, fh_ref, fl_ref, bh_ref, bl_ref, spaced, by_row):
    lat_rows = st_ref.shape[3]
    first = lax.axis_index("lat") * ROWS
    lane = lax.broadcasted_iota(jnp.int32, (8, 128), 1)
    wrapped = (lane % 16) >= 11
    spaced[...] = jnp.zeros_like(spaced)

    def one_basis(b, carry):
        for p in range(SPAN):
            spaced[0, 16 * p : 16 * p + SPAN, 0:lat_rows] = st_ref[b, p]
            for q in range(SPAN):
                r = 16 * p + q
                spaced[1, r : r + 1, 0:lat_rows] = st_ref[b, SPAN - 1 - p, SPAN - 1 - q : SPAN - q, :]
        by_row[0] = pltpu.roll(spaced[0].T, 128 - MARGIN, 1)
        moved = [pltpu.roll(spaced[1, 16 * p : 16 * p + 16, :], (MARGIN - p) % 128, 1) for p in range(8)]
        by_row[1] = pltpu.roll(jnp.concatenate(moved, axis=0).T, 128 - MARGIN, 1)

        def one_window(u, carry):
            for kind, hi_ref, lo_ref in ((0, fh_ref, fl_ref), (1, bh_ref, bl_ref)):
                rows = []
                for i01 in range(2):
                    line = by_row[kind, pl.ds(first + 2 * u + i01, 1), :]
                    line = jnp.broadcast_to(line, (8, 128))
                    shifted = pltpu.roll(line, 16 * i01, 1, stride=1, stride_axis=0)
                    rows.append(jnp.where(wrapped, pltpu.roll(shifted, 16, 1), shifted))
                hi, lo = split(jnp.concatenate(rows, axis=0))
                at = pl.ds(pl.multiple_of(16 * b, 16), 16)
                hi_ref[u, at, :] = hi
                lo_ref[u, at, :] = lo
            return carry

        return lax.fori_loop(0, WINDOWS, one_window, carry)

    lax.fori_loop(0, BASES, one_basis, 0)


def stencil_matrices(stencils):
    shape = jax.ShapeDtypeStruct((WINDOWS, 16 * BASES, 128), bf16)
    return pl.pallas_call(
        prep_kernel,
        out_shape=[shape] * 4,
        in_specs=[pl.BlockSpec(memory_space=pltpu.VMEM)],
        out_specs=[pl.BlockSpec(memory_space=pltpu.VMEM)] * 4,
        scratch_shapes=[pltpu.VMEM((2, 128, 128), f32), pltpu.VMEM((2, 128, 128), f32)],
        name="stencil_matrices",
    )(stencils)


def pack_tile(dst, tile, t, part, rows):
    if part == 0:
        dst[rows, 8 * t : 8 * t + 8, :] = tile
    else:
        base = dst.shape[1] - 16 + 8 * (t // 4)
        g = t % 4
        dst[rows, base : base + 8, 32 * g : 32 * g + 32] = tile


def tail_of(src, t, piece):
    base = src.shape[1] - 16 + 8 * (t // 4)
    g = t % 4
    return src[piece, base : base + 8, 32 * g : 32 * g + 32]


def step_kernel(
    members_ref, analysis_ref, fh_ref, fl_ref, bh_ref, bl_ref, mixing_ref,
    grad_ref, crps_ref,
    staged, m_hi, m_lo, e_hi, e_lo, s_hi, s_lo, field, damp, pack_r, pack_l,
    side, updown, corner, a_pack, c_pack, send1, recv1, send2, recv2,
    mix_sem, halo_send, halo_recv, a2a_send, a2a_recv,
):
    n_ens = lax.axis_size("ens")
    n_lat = lax.axis_size("lat")
    n_lon = lax.axis_size("lon")
    ens, lat, lon = lax.axis_index("ens"), lax.axis_index("lat"), lax.axis_index("lon")
    right, left = lax.rem(lon + 1, n_lon), lax.rem(lon + n_lon - 1, n_lon)
    has_up, has_down = lat > 0, lat < n_lat - 1
    channels = members_ref.shape[2]
    depth = BASES * channels
    tiles = channels // n_ens // 8

    for b in range(BASES):
        pltpu.make_async_copy(mixing_ref.at[b], staged.at[b], mix_sem.at[b]).start()

    barrier = pltpu.get_barrier_semaphore()

    def greet(k, carry):
        pl.semaphore_signal(barrier, 1, device_id={"ens": lax.rem(ens + k, n_ens)}, device_id_type=MESH)
        return carry

    lax.fori_loop(1, n_ens, greet, 0)
    for side_lon in (left, right):
        pl.semaphore_signal(barrier, 1, device_id={"lon": side_lon}, device_id_type=MESH)
    for there, other in ((has_up, lat - 1), (has_down, lat + 1)):
        @pl.when(there)
        def _():
            pl.semaphore_signal(barrier, 1, device_id={"lat": other}, device_id_type=MESH)
            for side_lon in (left, right):
                pl.semaphore_signal(barrier, 1, device_id={"lat": other, "lon": side_lon}, device_id_type=MESH)

    def fill_packs(src):
        for r in range(ROWS):
            pack_r[3 * r : 3 * r + 3, :] = src[r, COLS - MARGIN : COLS, :]
            pack_l[3 * r : 3 * r + 3, :] = src[r, 0:MARGIN, :]

    pack_r[56:64, :] = jnp.zeros((8, channels), f32)
    pack_l[56:64, :] = jnp.zeros((8, channels), f32)
    fill_packs(members_ref)
    pl.semaphore_wait(barrier, n_ens + 1 + 3 * has_up.astype(jnp.int32) + 3 * has_down.astype(jnp.int32))

    def halo_copies(phase, src):
        def remote(k, a, b, to):
            return pltpu.make_async_remote_copy(
                a, b, halo_send.at[phase, k], halo_recv.at[phase, k], device_id=to, device_id_type=MESH
            )

        up, down = lat - 1, lat + 1
        low = pl.ds(0, 16)
        high = pl.ds(48, 16)
        return [
            (None, None, remote(0, pack_r, side.at[phase, 0], {"lon": right})),
            (None, None, remote(1, pack_l, side.at[phase, 1], {"lon": left})),
            (has_down, has_up, remote(2, src.at[pl.ds(ROWS - 3, 3)], updown.at[phase, 0], {"lat": down})),
            (has_up, has_down, remote(3, src.at[pl.ds(0, 3)], updown.at[phase, 1], {"lat": up})),
            (has_down, has_up, remote(4, pack_r.at[high], corner.at[phase, 0], {"lat": down, "lon": right})),
            (has_down, has_up, remote(5, pack_l.at[high], corner.at[phase, 1], {"lat": down, "lon": left})),
            (has_up, has_down, remote(6, pack_r.at[low], corner.at[phase, 2], {"lat": up, "lon": right})),
            (has_up, has_down, remote(7, pack_l.at[low], corner.at[phase, 3], {"lat": up, "lon": left})),
        ]

    def start_halo(phase, src):
        for sends, _, copy in halo_copies(phase, src):
            if sends is None:
                copy.start()
            else:
                pl.when(sends)(copy.start)

    def put_row(r, inner, from_right, from_left):
        hi, lo = split(
            jnp.concatenate([inner, from_right, jnp.zeros((2, channels), f32), from_left], axis=0)
        )
        e_hi[16 * r : 16 * r + 16, :] = hi
        e_lo[16 * r : 16 * r + 16, :] = lo

    def extend(phase, src):
        copies = halo_copies(phase, src)
        for k in (0, 1):
            copies[k][2].wait()
        for r in range(ROWS):
            at = slice(3 * r, 3 * r + 3)
            put_row(r + MARGIN, src[r], side[phase, 1, at, :], side[phase, 0, at, :])
        for there, which, corners, first, offset in (
            (has_up, 0, (0, 1), 0, 3),
            (has_down, 1, (2, 3), ROWS + MARGIN, 0),
        ):
            @pl.when(there)
            def _():
                for k in (2 + which, 4 + 2 * which, 5 + 2 * which):
                    copies[k][2].wait_recv()
                for r in range(3):
                    at = slice(offset + 3 * r, offset + 3 * r + 3)
                    put_row(
                        first + r, updown[phase, which, r],
                        corner[phase, corners[1], at, :], corner[phase, corners[0], at, :],
                    )

            @pl.when(jnp.logical_not(there))
            def _():
                for ref in (e_hi, e_lo):
                    ref[16 * first : 16 * first + 48, :] = jnp.zeros((48, channels), bf16)
        for k in range(2, 8):
            pl.when(copies[k][0])(copies[k][2].wait_send)

    def stencil(w_hi, w_lo):
        def one_window(u, carry):
            at = pl.ds(pl.multiple_of(32 * u, 32), 128)
            x_hi, x_lo = e_hi[at, :], e_lo[at, :]
            wh = w_hi[u]
            out = mm(jnp.concatenate([wh, wh], axis=1), jnp.concatenate([x_hi, x_lo], axis=0)) + mm(w_lo[u], x_hi)
            hi, lo = split(out)
            to = pl.ds(pl.multiple_of(16 * u, 16), 16)
            for b in range(BASES):
                s_hi[to, b * channels : (b + 1) * channels] = hi[16 * b : 16 * b + 16]
                s_lo[to, b * channels : (b + 1) * channels] = lo[16 * b : 16 * b + 16]
            return carry

        lax.fori_loop(0, WINDOWS, one_window, 0)

    def mix(cols):
        weights = m_hi[:, cols]
        return mm(s_hi[...], weights) + mm(s_lo[...], weights) + mm(s_hi[...], m_lo[:, cols])

    def chunks():
        return [slice(c, min(c + 256, channels)) for c in range(0, channels, 256)]

    def load_weights(b, carry):
        pltpu.make_async_copy(mixing_ref.at[b], staged.at[b], mix_sem.at[b]).wait()

        def part(k, carry):
            rows = pl.ds(pl.multiple_of(128 * k, 128), 128)
            hi, lo = split(staged[b, rows, :])
            to = pl.ds(pl.multiple_of(b * channels + 128 * k, 128), 128)
            m_hi[to, :] = hi
            m_lo[to, :] = lo
            return carry

        return lax.fori_loop(0, channels // 128, part, carry)

    def transpose_weights(b, carry):
        def part(k, carry):
            cols = pl.ds(pl.multiple_of(128 * k, 128), 128)
            hi, lo = split(staged[b, :, cols].T)
            to = pl.ds(pl.multiple_of(b * channels + 128 * k, 128), 128)
            m_hi[to, :] = hi
            m_lo[to, :] = lo
            return carry

        return lax.fori_loop(0, channels // 128, part, carry)

    start_halo(0, members_ref)

    zero_piece = jnp.zeros((16, 128), f32)
    a_pack[0, 8 * tiles : 8 * tiles + 16, :] = zero_piece
    truth = jnp.concatenate(
        [analysis_ref[...].reshape(ROWS * COLS, 8 * tiles), jnp.zeros((ROWS * COLS, 128 - 8 * tiles), f32)], axis=1
    )
    main, tail = truth[:128].T, jnp.concatenate([truth[128:], jnp.zeros((96, 128), f32)], axis=0).T
    for t in range(tiles):
        pack_tile(a_pack, main[8 * t : 8 * t + 8], t, 0, 0)
        pack_tile(a_pack, tail[8 * t : 8 * t + 8, 0:32], t, 1, 0)

    lax.fori_loop(0, BASES, load_weights, 0)
    extend(0, members_ref)
    stencil(fh_ref, fl_ref)

    for d in range(n_ens):
        send1[d, 8 * tiles : 8 * tiles + 16, :] = zero_piece
    for cols in chunks():
        width = cols.stop - cols.start
        activation = jnp.tanh(mix(cols))
        damp[:, cols] = 1.0 - activation * activation
        forecast = members_ref[:, :, cols].reshape(ROWS * COLS, width) + activation
        for c in range(width // 128):
            part = forecast[:, 128 * c : 128 * c + 128]
            main = part[:128].T
            tail = jnp.concatenate([part[128:], jnp.zeros((96, 128), f32)], axis=0).T
            for s in range(16):
                k = (cols.start // 128 + c) * 16 + s
                pack_tile(send1, main[8 * s : 8 * s + 8], k % tiles, 0, k // tiles)
                pack_tile(send1, tail[8 * s : 8 * s + 8, 0:32], k % tiles, 1, k // tiles)

    def exchange(phase, src, dst, other, slot):
        return pltpu.make_async_remote_copy(
            src.at[other], dst.at[slot], a2a_send.at[phase, other], a2a_recv.at[phase, slot],
            device_id={"ens": other}, device_id_type=MESH,
        )

    def start_all(phase, src, dst):
        def start(k, carry):
            exchange(phase, src, dst, lax.rem(ens + k, n_ens), ens).start()
            return carry

        lax.fori_loop(1, n_ens, start, 0)
        dst[ens] = src[ens]

    def wait_all(phase, src, dst):
        def wait(k, carry):
            other = lax.rem(ens + k, n_ens)
            exchange(phase, src, dst, other, other).wait_recv()
            exchange(phase, src, dst, other, ens).wait_send()
            return carry

        lax.fori_loop(1, n_ens, wait, 0)

    start_all(0, send1, recv1)
    lax.fori_loop(0, BASES, transpose_weights, 0)
    wait_all(0, send1, recv1)

    members_total = n_ens
    diagonal = members_total * float(np.sqrt(np.float32(SMOOTH)))
    pairs_scale = 2.0 * members_total * (members_total - 1)

    def score(t, carry):
        rows = pl.ds(pl.multiple_of(8 * t, 8), 8)
        truth = a_pack[0, rows, :]
        x = [recv1[m, rows, :] - truth for m in range(n_ens)]
        slope = [None] * n_ens
        own, pair_abs = None, None
        for m in range(n_ens):
            for n in range(m + 1, n_ens):
                d = x[m] - x[n]
                s2 = d * d + SMOOTH
                r = lax.rsqrt(s2)
                sl = d * r
                ab = s2 * r
                pair_abs = ab if pair_abs is None else pair_abs + ab
                slope[m] = sl if slope[m] is None else slope[m] + sl
                slope[n] = -sl if slope[n] is None else slope[n] - sl
            s2 = x[m] * x[m] + SMOOTH
            r = lax.rsqrt(s2)
            own = s2 * r if own is None else own + s2 * r
            send2[m, rows, :] = x[m] * r - slope[m] * (1.0 / (members_total - 1.0))
        c_pack[0, rows, :] = own * (1.0 / members_total) - (2.0 * pair_abs + diagonal) * (1.0 / pairs_scale)
        return carry

    lax.fori_loop(0, tiles + 2, score, 0)
    start_all(1, send2, recv2)

    main = jnp.concatenate(
        [c_pack[0, 8 * t : 8 * t + 8, :] for t in range(tiles)] + [jnp.zeros((128 - 8 * tiles, 128), f32)], axis=0
    ).T
    crps_ref[0:16] = main[:, 0 : 8 * tiles].reshape(16, COLS, 8 * tiles)
    tail = jnp.concatenate([tail_of(c_pack, t, 0) for t in range(tiles)], axis=0)
    tail = jnp.concatenate([tail, jnp.zeros((8 * tiles, 96), f32)], axis=1)
    tail = jnp.concatenate([tail, jnp.zeros((128 - 8 * tiles, 128), f32)], axis=0).T
    crps_ref[16:20] = tail[0:32, 0 : 8 * tiles].reshape(4, COLS, 8 * tiles)

    wait_all(1, send2, recv2)

    for c in range(channels // 128):
        mains, tails = [], []
        for s in range(16):
            k = c * 16 + s
            piece, t = k // tiles, k % tiles
            mains.append(recv2[piece, 8 * t : 8 * t + 8, :])
            tails.append(tail_of(recv2, t, piece))
        main = jnp.concatenate(mains, axis=0).T
        tail = jnp.concatenate([jnp.concatenate(tails, axis=0), jnp.zeros((128, 96), f32)], axis=1).T
        cols = slice(128 * c, 128 * c + 128)
        grad_ref[0:16, :, cols] = main.reshape(16, COLS, 128)
        grad_ref[16:20, :, cols] = tail[0:32].reshape(4, COLS, 128)
    field[...] = grad_ref[...] * damp[...].reshape(ROWS, COLS, channels)
    fill_packs(field)
    start_halo(1, field)
    extend(1, field)
    stencil(bh_ref, bl_ref)
    for cols in chunks():
        width = cols.stop - cols.start
        grad_ref[:, :, cols] = grad_ref[:, :, cols] + mix(cols).reshape(ROWS, COLS, width)


def local(members, analysis, stencils, mixing):
    channels = members.shape[3]
    n_ens = lax.axis_size("ens")
    per = channels // n_ens
    depth = BASES * channels
    cells = ROWS * COLS
    piece = (n_ens, per + 16, 128)
    matrices = stencil_matrices(stencils)
    vmem = pl.BlockSpec(memory_space=pltpu.VMEM)
    grad, crps = pl.pallas_call(
        step_kernel,
        out_shape=[
            jax.ShapeDtypeStruct((ROWS, COLS, channels), f32),
            jax.ShapeDtypeStruct((ROWS, COLS, per), f32),
        ],
        in_specs=[vmem] * 6 + [pl.BlockSpec(memory_space=pl.ANY)],
        out_specs=[vmem, vmem],
        scratch_shapes=[
            pltpu.VMEM((BASES, channels, channels), f32),
            pltpu.VMEM((depth, channels), bf16),
            pltpu.VMEM((depth, channels), bf16),
            pltpu.VMEM((16 * EXT, channels), bf16),
            pltpu.VMEM((16 * EXT, channels), bf16),
            pltpu.VMEM((cells, depth), bf16),
            pltpu.VMEM((cells, depth), bf16),
            pltpu.VMEM((ROWS, COLS, channels), f32),
            pltpu.VMEM((cells, channels), f32),
            pltpu.VMEM((64, channels), f32),
            pltpu.VMEM((64, channels), f32),
            pltpu.VMEM((2, 2, 64, channels), f32),
            pltpu.VMEM((2, 2, MARGIN, COLS, channels), f32),
            pltpu.VMEM((2, 4, 16, channels), f32),
            pltpu.VMEM((1, per + 16, 128), f32),
            pltpu.VMEM((1, per + 16, 128), f32),
            pltpu.VMEM(piece, f32),
            pltpu.VMEM(piece, f32),
            pltpu.VMEM(piece, f32),
            pltpu.VMEM(piece, f32),
            pltpu.SemaphoreType.DMA((BASES,)),
            pltpu.SemaphoreType.DMA((2, 8)),
            pltpu.SemaphoreType.DMA((2, 8)),
            pltpu.SemaphoreType.DMA((2, n_ens)),
            pltpu.SemaphoreType.DMA((2, n_ens)),
        ],
        compiler_params=pltpu.CompilerParams(
            collective_id=0, has_side_effects=True, vmem_limit_bytes=56 * 1024 * 1024
        ),
        name="ensemble_step",
    )(members[0], analysis, *matrices, mixing)
    return grad[None], crps


def solution(mesh):
    in_specs = (P("ens", "lat", "lon", None), P("lat", "lon", "ens"), P(), P())
    out_specs = (P("ens", "lat", "lon", None), P("lat", "lon", "ens"))
    return jax.shard_map(local, mesh=mesh, in_specs=in_specs, out_specs=out_specs, check_vma=False)
```

time: 515 us -> 87.3 us (0.17); the launches traced: 505 us -> 85.8 us
  waiting for transfers between devices: 273 us -> 0 us
  Pallas kernels: 0 us -> 81.8 us
  local copies, waits for them, and re-layouts: 81.4 us -> 3.31 us
  blocking collectives: 53.7 us -> 0 us
  other arithmetic: 46.9 us -> 0 us
  matrix products: 21 us -> 0 us
  between operations: 15.4 us -> 0.64 us
  starting transfers between devices: 13.9 us -> 0 us
    unnamed x3 -> x0, waiting for transfers between devices: 146 us -> none
    all_gather x1 -> x0, waiting for transfers between devices: 120 us -> none  [local(): lax.all_gather(prediction_error, 'ens', axis=0, tiled=True)[None]]
    pallas_call x0 -> x2, Pallas kernels: none -> 81.8 us  [the longest x1 67.5 us: local(): pl.pallas_call(step_kernel, out_shape=[jax.ShapeDtypeStruct((ROWS, COLS,...]
    mul x112 -> x0, local copies, waits for them, and re-layouts: 62 us -> none  [apply_taps(): weights[:, tap_index, None, :, None, None]]
    all_gather x1 -> x0, blocking collectives: 53.7 us -> none  [local(): observed_truth = lax.all_gather(analysis, 'ens', axis=2, tiled=True)]
    dot_general x2 -> x0, matrix products: 21 us -> none  [the longest x1 12.2 us: local(): lax.dot_general(spread.reshape(-1, BASES, channels), mixing, (((1, 2), (0...]
    dot_general x1 -> x0, other arithmetic: 20.4 us -> none  [local(): lax.dot_general(spread.reshape(-1, BASES, channels), mixing, (((1, 2), (0...]
    add x1 -> x0, other arithmetic: 18.8 us -> none  [apply_taps(): running + weights[:, tap_index, None, :, None, None] * extended[None, :,...]
  transfers between devices with their start and end apart: 10 -> 0, of which waited for: 6 -> 0; matrix products, arithmetic and copies ran while one was open for 21% -> 0% of each run, Pallas kernels for 0% -> 0%
where the time goes in v1:
time: 87.3 us; the launch traced here: 85.8 us
  Pallas kernels  81.8 us (94%)
  local copies, waits for them, and re-layouts  3.31 us (4%)
    pallas_call x1, Pallas kernels, local(): pl.pallas_call(step_kernel, out_shape=[jax.ShapeDtypeStruct((ROWS, COLS,...  67.5 us
    pallas_call x1, Pallas kernels, stencil_matrices(): pl.pallas_call(prep_kernel, out_shape=[shape] * 4, in_specs=[pl.BlockSpec...  14.3 us
    unnamed x2, local copies, waits for them, and re-layouts  3.31 us

profile of v1, /device:TPU:1, one launch (start us, length us, event | category | flops | bytes accessed | tf_op | source)
XLA Modules:
  0.0 85.8 jit_solution(16002905738839610739)
XLA Ops:
  0.6 14.3 %stencil_matrices.1 = (bf16[10,112,128]{2,1,0:T(8,128)(2,1)}, bf16[10,112,128]{2,1,0:T(8,128)(2,1)}, bf16[10,112,128]{2,1,0:T(8,128)(2,1)}, bf16[10,112,128]{2,1,0:T(8,128)(2,1)}) custom-call(f32[7,7,7,80]{3,2,1,0:T(8,128)} %st_ref.1), custom_call_target="tpu_custom_call" | custom-call | tf_op jit(solution)/shard_map/stencil_matrices/pallas_call | solution.py:71
  14.9 67.5 %ensemble_step.1 = (f32[20,8,640]{2,1,0:T(8,128)}, f32[20,8,40]{2,1,0:T(8,128)}) custom-call(f32[20,8,640]{2,1,0:T(8,128)} %bitcast.3, f32[20,8,40]{2,1,0:T(8,128)} %analysis_ref.1, bf16[10,112,128]{2,1,0:T(8,128)(2,1)} %get-tuple-element.8.fh_ref, bf16[10,112,128]{2,1,0:T(8,128)(2,1)} %get-tuple-element.9.fl_ref, ...), custom_call_target="tpu_custom_call" | custom-call | tf_op jit(solution)/shard_map/ensemble_step/pallas_call | solution.py:382
  82.5 1.8 %copy.8 = f32[1,20,8,640]{3,2,1,0:T(8,128)} copy(f32[1,20,8,640]{3,2,1,0:T(8,128)} %bitcast.2) | data formatting | bytes 819200
  84.3 1.5 %copy.9 = f32[20,8,40]{2,1,0:T(8,128)} copy(f32[20,8,40]{2,1,0:T(8,128)} %get-tuple-element.17) | data formatting | bytes 51200

commit v2 on v1

--- a/solution.py
+++ b/solution.py
@@ -30,7 +30,7 @@
     return jnp.dot(a, b, preferred_element_type=f32)
 
 
-def prep_kernel(st_ref, fh_ref, fl_ref, bh_ref, bl_ref, spaced, by_row):
+def stencil_matrices(kind, st_ref, hi_ref, lo_ref, spaced, by_row):
     lat_rows = st_ref.shape[3]
     first = lax.axis_index("lat") * ROWS
     lane = lax.broadcasted_iota(jnp.int32, (8, 128), 1)
@@ -39,43 +39,30 @@
 
     def one_basis(b, carry):
         for p in range(SPAN):
-            spaced[0, 16 * p : 16 * p + SPAN, 0:lat_rows] = st_ref[b, p]
-            for q in range(SPAN):
-                r = 16 * p + q
-                spaced[1, r : r + 1, 0:lat_rows] = st_ref[b, SPAN - 1 - p, SPAN - 1 - q : SPAN - q, :]
-        by_row[0] = pltpu.roll(spaced[0].T, 128 - MARGIN, 1)
-        moved = [pltpu.roll(spaced[1, 16 * p : 16 * p + 16, :], (MARGIN - p) % 128, 1) for p in range(8)]
-        by_row[1] = pltpu.roll(jnp.concatenate(moved, axis=0).T, 128 - MARGIN, 1)
-
-        def one_window(u, carry):
-            for kind, hi_ref, lo_ref in ((0, fh_ref, fl_ref), (1, bh_ref, bl_ref)):
-                rows = []
-                for i01 in range(2):
-                    line = by_row[kind, pl.ds(first + 2 * u + i01, 1), :]
-                    line = jnp.broadcast_to(line, (8, 128))
-                    shifted = pltpu.roll(line, 16 * i01, 1, stride=1, stride_axis=0)
-                    rows.append(jnp.where(wrapped, pltpu.roll(shifted, 16, 1), shifted))
-                hi, lo = split(jnp.concatenate(rows, axis=0))
-                at = pl.ds(pl.multiple_of(16 * b, 16), 16)
-                hi_ref[u, at, :] = hi
-                lo_ref[u, at, :] = lo
-            return carry
-
-        return lax.fori_loop(0, WINDOWS, one_window, carry)
+            if kind == 0:
+                spaced[16 * p : 16 * p + SPAN, 0:lat_rows] = st_ref[b, p]
+            else:
+                for q in range(SPAN):
+                    r = 16 * p + q
+                    spaced[r : r + 1, 0:lat_rows] = st_ref[b, SPAN - 1 - p, SPAN - 1 - q : SPAN - q, :]
+        if kind == 0:
+            lines = spaced[...]
+        else:
+            lines = jnp.concatenate(
+                [pltpu.roll(spaced[16 * p : 16 * p + 16, :], (MARGIN - p) % 128, 1) for p in range(8)], axis=0
+            )
+        by_row[...] = pltpu.roll(lines.T, 128 - MARGIN, 1)
+        at = pl.ds(pl.multiple_of(16 * b, 16), 16)
+        for u in range(WINDOWS):
+            rows = []
+            for i01 in range(2):
+                line = jnp.broadcast_to(by_row[pl.ds(first + 2 * u + i01, 1), :], (8, 128))
+                shifted = pltpu.roll(line, 16 * i01, 1, stride=1, stride_axis=0)
+                rows.append(jnp.where(wrapped, pltpu.roll(shifted, 16, 1), shifted))
+            hi_ref[u, at, :], lo_ref[u, at, :] = split(jnp.concatenate(rows, axis=0))
+        return carry
 
     lax.fori_loop(0, BASES, one_basis, 0)
-
-
-def stencil_matrices(stencils):
-    shape = jax.ShapeDtypeStruct((WINDOWS, 16 * BASES, 128), bf16)
-    return pl.pallas_call(
-        prep_kernel,
-        out_shape=[shape] * 4,
-        in_specs=[pl.BlockSpec(memory_space=pltpu.VMEM)],
-        out_specs=[pl.BlockSpec(memory_space=pltpu.VMEM)] * 4,
-        scratch_shapes=[pltpu.VMEM((2, 128, 128), f32), pltpu.VMEM((2, 128, 128), f32)],
-        name="stencil_matrices",
-    )(stencils)
 
 
 def pack_tile(dst, tile, t, part, rows):
@@ -94,9 +81,9 @@
 
 
 def step_kernel(
-    members_ref, analysis_ref, fh_ref, fl_ref, bh_ref, bl_ref, mixing_ref,
+    members_ref, analysis_ref, stencils_ref, mixing_ref,
     grad_ref, crps_ref,
-    staged, m_hi, m_lo, e_hi, e_lo, s_hi, s_lo, field, damp, pack_r, pack_l,
+    w_hi, w_lo, spaced, by_row, staged, m_hi, m_lo, e_hi, e_lo, s_hi, s_lo, field, damp, pack_r, pack_l,
     side, updown, corner, a_pack, c_pack, send1, recv1, send2, recv2,
     mix_sem, halo_send, halo_recv, a2a_send, a2a_recv,
 ):
@@ -202,7 +189,7 @@
         for k in range(2, 8):
             pl.when(copies[k][0])(copies[k][2].wait_send)
 
-    def stencil(w_hi, w_lo):
+    def stencil():
         def one_window(u, carry):
             at = pl.ds(pl.multiple_of(32 * u, 32), 128)
             x_hi, x_lo = e_hi[at, :], e_lo[at, :]
@@ -215,7 +202,7 @@
                 s_lo[to, b * channels : (b + 1) * channels] = lo[16 * b : 16 * b + 16]
             return carry
 
-        lax.fori_loop(0, WINDOWS, one_window, 0)
+        lax.fori_loop(0, WINDOWS, one_window, 0, unroll=True)
 
     def mix(cols):
         weights = m_hi[:, cols]
@@ -235,7 +222,7 @@
             m_lo[to, :] = lo
             return carry
 
-        return lax.fori_loop(0, channels // 128, part, carry)
+        return lax.fori_loop(0, channels // 128, part, carry, unroll=True)
 
     def transpose_weights(b, carry):
         def part(k, carry):
@@ -246,9 +233,10 @@
             m_lo[to, :] = lo
             return carry
 
-        return lax.fori_loop(0, channels // 128, part, carry)
+        return lax.fori_loop(0, channels // 128, part, carry, unroll=True)
 
     start_halo(0, members_ref)
+    stencil_matrices(0, stencils_ref, w_hi, w_lo, spaced, by_row)
 
     zero_piece = jnp.zeros((16, 128), f32)
     a_pack[0, 8 * tiles : 8 * tiles + 16, :] = zero_piece
@@ -262,7 +250,7 @@
 
     lax.fori_loop(0, BASES, load_weights, 0)
     extend(0, members_ref)
-    stencil(fh_ref, fl_ref)
+    stencil()
 
     for d in range(n_ens):
         send1[d, 8 * tiles : 8 * tiles + 16, :] = zero_piece
@@ -304,6 +292,7 @@
         lax.fori_loop(1, n_ens, wait, 0)
 
     start_all(0, send1, recv1)
+    stencil_matrices(1, stencils_ref, w_hi, w_lo, spaced, by_row)
     lax.fori_loop(0, BASES, transpose_weights, 0)
     wait_all(0, send1, recv1)
 
@@ -364,7 +353,7 @@
     fill_packs(field)
     start_halo(1, field)
     extend(1, field)
-    stencil(bh_ref, bl_ref)
+    stencil()
     for cols in chunks():
         width = cols.stop - cols.start
         grad_ref[:, :, cols] = grad_ref[:, :, cols] + mix(cols).reshape(ROWS, COLS, width)
@@ -377,7 +366,6 @@
     depth = BASES * channels
     cells = ROWS * COLS
     piece = (n_ens, per + 16, 128)
-    matrices = stencil_matrices(stencils)
     vmem = pl.BlockSpec(memory_space=pltpu.VMEM)
     grad, crps = pl.pallas_call(
         step_kernel,
@@ -385,9 +373,13 @@
             jax.ShapeDtypeStruct((ROWS, COLS, channels), f32),
             jax.ShapeDtypeStruct((ROWS, COLS, per), f32),
         ],
-        in_specs=[vmem] * 6 + [pl.BlockSpec(memory_space=pl.ANY)],
+        in_specs=[vmem] * 3 + [pl.BlockSpec(memory_space=pl.ANY)],
         out_specs=[vmem, vmem],
         scratch_shapes=[
+            pltpu.VMEM((WINDOWS, 16 * BASES, 128), bf16),
+            pltpu.VMEM((WINDOWS, 16 * BASES, 128), bf16),
+            pltpu.VMEM((128, 128), f32),
+            pltpu.VMEM((128, 128), f32),
             pltpu.VMEM((BASES, channels, channels), f32),
             pltpu.VMEM((depth, channels), bf16),
             pltpu.VMEM((depth, channels), bf16),
@@ -418,7 +410,7 @@
             collective_id=0, has_side_effects=True, vmem_limit_bytes=56 * 1024 * 1024
         ),
         name="ensemble_step",
-    )(members[0], analysis, *matrices, mixing)
+    )(members[0], analysis, stencils, mixing)
     return grad[None], crps
 
 

time: 87.3 us -> 69.8 us (0.80)
  the two profiles are of different devices: /device:TPU:1 before, /device:TPU:5 now
where the time goes in v2:
time: 69.8 us; the launch traced here: 69.6 us
  Pallas kernels  65.6 us (94%)
  local copies, waits for them, and re-layouts  3.31 us (5%)
    pallas_call x1, Pallas kernels, local(): pl.pallas_call(step_kernel, out_shape=[jax.ShapeDtypeStruct((ROWS, COLS,...  65.6 us
    unnamed x2, local copies, waits for them, and re-layouts  3.31 us

profile of v2, /device:TPU:5, one launch (start us, length us, event | category | flops | bytes accessed | tf_op | source)
XLA Modules:
  0.0 69.6 jit_solution(3737152546848904983)
XLA Ops:
  0.6 65.6 %ensemble_step.1 = (f32[20,8,640]{2,1,0:T(8,128)}, f32[20,8,40]{2,1,0:T(8,128)}) custom-call(f32[20,8,640]{2,1,0:T(8,128)} %bitcast.3, f32[20,8,40]{2,1,0:T(8,128)} %analysis_ref.1, f32[7,7,7,80]{3,2,1,0:T(8,128)} %stencils_ref.1, f32[7,640,640]{2,1,0:T(8,128)} %mixing_ref.1), custom_call_target="tpu_custom_call" | custom-call | tf_op jit(solution)/shard_map/ensemble_step/pallas_call | solution.py:370
  66.3 1.8 %copy.8 = f32[1,20,8,640]{3,2,1,0:T(8,128)} copy(f32[1,20,8,640]{3,2,1,0:T(8,128)} %bitcast.2) | data formatting | bytes 819200
  68.1 1.5 %copy.9 = f32[20,8,40]{2,1,0:T(8,128)} copy(f32[20,8,40]{2,1,0:T(8,128)} %get-tuple-element.9) | data formatting | bytes 51200

commit v3 on v2

v3 whole, which is shorter than its diff:
```python
import functools

import jax
import jax.numpy as jnp
import numpy as np
from jax import lax
from jax.experimental import pallas as pl
from jax.experimental.pallas import tpu as pltpu
from jax.sharding import PartitionSpec as P

BASES = 7
SPAN = 7
MARGIN = 3
ROWS = 20
COLS = 8
WINDOWS = ROWS // 2
EXT = ROWS + 2 * MARGIN
SMOOTH = 0.01
MESH = pl.DeviceIdType.MESH
f32 = jnp.float32
bf16 = jnp.bfloat16


def split(x):
    hi = x.astype(bf16)
    return hi, (x - hi.astype(f32)).astype(bf16)


def mm(a, b):
    return jnp.dot(a, b, preferred_element_type=f32)


def stencil_matrices(kind, st_ref, hi_ref, lo_ref, spaced, by_row):
    lat_rows = st_ref.shape[3]
    first = lax.axis_index("lat") * ROWS
    lane = lax.broadcasted_iota(jnp.int32, (8, 128), 1)
    wrapped = (lane % 16) >= 11
    spaced[...] = jnp.zeros_like(spaced)

    def one_basis(b, carry):
        for p in range(SPAN):
            if kind == 0:
                spaced[16 * p : 16 * p + SPAN, 0:lat_rows] = st_ref[b, p]
            else:
                for q in range(SPAN):
                    r = 16 * p + q
                    spaced[r : r + 1, 0:lat_rows] = st_ref[b, SPAN - 1 - p, SPAN - 1 - q : SPAN - q, :]
        if kind == 0:
            lines = spaced[...]
        else:
            lines = jnp.concatenate(
                [pltpu.roll(spaced[16 * p : 16 * p + 16, :], (MARGIN - p) % 128, 1) for p in range(8)], axis=0
            )
        by_row[...] = pltpu.roll(lines.T, 128 - MARGIN, 1)
        at = pl.ds(pl.multiple_of(16 * b, 16), 16)
        for u in range(WINDOWS):
            rows = []
            for i01 in range(2):
                line = jnp.broadcast_to(by_row[pl.ds(first + 2 * u + i01, 1), :], (8, 128))
                shifted = pltpu.roll(line, 16 * i01, 1, stride=1, stride_axis=0)
                rows.append(jnp.where(wrapped, pltpu.roll(shifted, 16, 1), shifted))
            hi_ref[u, at, :], lo_ref[u, at, :] = split(jnp.concatenate(rows, axis=0))
        return carry

    lax.fori_loop(0, BASES, one_basis, 0)


TILES = 5
BODY = 8 * (TILES + 1)
STEPS = ((0, 1), (2, 3), (4,))
STEP_ROWS = ((0, 24), (24, 16), (40, 8))


def spread_rest(tails, rest):
    for c in range(8):
        lanes = slice(32 * (c % 4), 32 * (c % 4) + 32)
        rest[:, c // 4, lanes] = tails[:, c, 0:32]


def gather_rest(rest, tails):
    for c in range(8):
        lanes = slice(32 * (c % 4), 32 * (c % 4) + 32)
        tails[:, c, 0:32] = rest[:, c // 4, lanes]


def padded(x, rows, lanes):
    if x.shape[1] < lanes:
        x = jnp.concatenate([x, jnp.zeros((x.shape[0], lanes - x.shape[1]), f32)], axis=1)
    if x.shape[0] < rows:
        x = jnp.concatenate([x, jnp.zeros((rows - x.shape[0], lanes), f32)], axis=0)
    return x


def step_kernel(
    members_ref, analysis_ref, stencils_ref, mixing_ref,
    grad_ref, crps_ref,
    w_hi, w_lo, spaced, by_row, staged, turned, m_hi, m_lo, e_hi, e_lo, s_hi, s_lo,
    field, act, damp_main, damp_tail, pack_r, pack_l, side, updown, corner,
    a_body, a_rest, c_body, c_rest, tails, send1, rest1, recv1, got1, send2, rest2, recv2, got2,
    mix_sem, halo_send, halo_recv, a2a_send, a2a_recv,
):
    n_ens = lax.axis_size("ens")
    n_lat = lax.axis_size("lat")
    n_lon = lax.axis_size("lon")
    ens, lat, lon = lax.axis_index("ens"), lax.axis_index("lat"), lax.axis_index("lon")
    right, left = lax.rem(lon + 1, n_lon), lax.rem(lon + n_lon - 1, n_lon)
    has_up, has_down = lat > 0, lat < n_lat - 1
    channels = members_ref.shape[2]
    cells = ROWS * COLS
    per = 8 * TILES

    for b in range(BASES):
        pltpu.make_async_copy(mixing_ref.at[b], staged.at[b], mix_sem.at[b]).start()

    barrier = pltpu.get_barrier_semaphore()

    def greet(k, carry):
        pl.semaphore_signal(barrier, 1, device_id={"ens": lax.rem(ens + k, n_ens)}, device_id_type=MESH)
        return carry

    lax.fori_loop(1, n_ens, greet, 0)
    for side_lon in (left, right):
        pl.semaphore_signal(barrier, 1, device_id={"lon": side_lon}, device_id_type=MESH)
    for there, other in ((has_up, lat - 1), (has_down, lat + 1)):
        @pl.when(there)
        def _():
            pl.semaphore_signal(barrier, 1, device_id={"lat": other}, device_id_type=MESH)
            for side_lon in (left, right):
                pl.semaphore_signal(barrier, 1, device_id={"lat": other, "lon": side_lon}, device_id_type=MESH)

    def fill_packs(src, cols):
        for r in range(ROWS):
            pack_r[3 * r : 3 * r + 3, cols] = src[r, COLS - MARGIN : COLS, cols]
            pack_l[3 * r : 3 * r + 3, cols] = src[r, 0:MARGIN, cols]

    every = slice(0, channels)
    pack_r[56:64, :] = jnp.zeros((8, channels), f32)
    pack_l[56:64, :] = jnp.zeros((8, channels), f32)
    fill_packs(members_ref, every)
    pl.semaphore_wait(barrier, n_ens + 1 + 3 * has_up.astype(jnp.int32) + 3 * has_down.astype(jnp.int32))

    def halo_copies(phase, src, cols):
        back = min(phase, 1)
        lanes = pl.ds(cols.start, cols.stop - cols.start)

        def remote(k, a, b, to):
            return pltpu.make_async_remote_copy(
                a, b, halo_send.at[phase, k], halo_recv.at[phase, k], device_id=to, device_id_type=MESH
            )

        up, down = lat - 1, lat + 1
        low = pl.ds(0, 16)
        high = pl.ds(48, 16)
        return [
            (None, None, remote(0, pack_r.at[:, lanes], side.at[back, 0, :, lanes], {"lon": right})),
            (None, None, remote(1, pack_l.at[:, lanes], side.at[back, 1, :, lanes], {"lon": left})),
            (
                has_down, has_up,
                remote(2, src.at[pl.ds(ROWS - 3, 3), :, lanes], updown.at[back, 0, :, :, lanes], {"lat": down}),
            ),
            (
                has_up, has_down,
                remote(3, src.at[pl.ds(0, 3), :, lanes], updown.at[back, 1, :, :, lanes], {"lat": up}),
            ),
            (
                has_down, has_up,
                remote(4, pack_r.at[high, lanes], corner.at[back, 0, :, lanes], {"lat": down, "lon": right}),
            ),
            (
                has_down, has_up,
                remote(5, pack_l.at[high, lanes], corner.at[back, 1, :, lanes], {"lat": down, "lon": left}),
            ),
            (
                has_up, has_down,
                remote(6, pack_r.at[low, lanes], corner.at[back, 2, :, lanes], {"lat": up, "lon": right}),
            ),
            (
                has_up, has_down,
                remote(7, pack_l.at[low, lanes], corner.at[back, 3, :, lanes], {"lat": up, "lon": left}),
            ),
        ]

    def start_halo(phase, src, cols):
        for sends, _, copy in halo_copies(phase, src, cols):
            if sends is None:
                copy.start()
            else:
                pl.when(sends)(copy.start)

    def put_row(r, inner, from_right, from_left, cols):
        gap = jnp.zeros((2, cols.stop - cols.start), f32)
        hi, lo = split(jnp.concatenate([inner, from_right, gap, from_left], axis=0))
        e_hi[16 * r : 16 * r + 16, cols] = hi
        e_lo[16 * r : 16 * r + 16, cols] = lo

    def extend(phase, src, cols):
        copies = halo_copies(phase, src, cols)
        back = min(phase, 1)
        for k in (0, 1):
            copies[k][2].wait()
        for r in range(ROWS):
            at = slice(3 * r, 3 * r + 3)
            put_row(r + MARGIN, src[r, :, cols], side[back, 1, at, cols], side[back, 0, at, cols], cols)
        for there, which, corners, first, offset in (
            (has_up, 0, (0, 1), 0, 3),
            (has_down, 1, (2, 3), ROWS + MARGIN, 0),
        ):
            @pl.when(there)
            def _():
                for k in (2 + which, 4 + 2 * which, 5 + 2 * which):
                    copies[k][2].wait_recv()
                for r in range(3):
                    at = slice(offset + 3 * r, offset + 3 * r + 3)
                    put_row(
                        first + r, updown[back, which, r, :, cols],
                        corner[back, corners[1], at, cols], corner[back, corners[0], at, cols], cols,
                    )

            @pl.when(jnp.logical_not(there))
            def _():
                for ref in (e_hi, e_lo):
                    ref[16 * first : 16 * first + 48, cols] = jnp.zeros((48, cols.stop - cols.start), bf16)
        for k in range(2, 8):
            pl.when(copies[k][0])(copies[k][2].wait_send)

    def stencil(cols):
        width = cols.stop - cols.start

        def one_window(u, carry):
            at = pl.ds(pl.multiple_of(32 * u, 32), 128)
            x_hi, x_lo = e_hi[at, cols], e_lo[at, cols]
            wh = w_hi[u]
            out = mm(jnp.concatenate([wh, wh], axis=1), jnp.concatenate([x_hi, x_lo], axis=0)) + mm(w_lo[u], x_hi)
            hi, lo = split(out)
            to = pl.ds(pl.multiple_of(16 * u, 16), 16)
            for b in range(BASES):
                here = slice(BASES * cols.start + b * width, BASES * cols.start + (b + 1) * width)
                s_hi[to, here] = hi[16 * b : 16 * b + 16]
                s_lo[to, here] = lo[16 * b : 16 * b + 16]
            return carry

        lax.fori_loop(0, WINDOWS, one_window, 0, unroll=True)

    def mix(cols, inputs):
        k = slice(BASES * inputs.start, BASES * inputs.stop)
        weights = m_hi[k, cols]
        return mm(s_hi[:, k], weights) + mm(s_lo[:, k], weights) + mm(s_hi[:, k], m_lo[k, cols])

    def chunks():
        return [slice(c, min(c + 256, channels)) for c in range(0, channels, 256)]

    def load_weights(b, carry):
        pltpu.make_async_copy(mixing_ref.at[b], staged.at[b], mix_sem.at[b]).wait()
        for k in range(channels // 128):
            hi, lo = split(staged[b, 128 * k : 128 * k + 128, :])
            to = pl.ds(pl.multiple_of(b * channels + 128 * k, 128), 128)
            m_hi[to, :] = hi
            m_lo[to, :] = lo
        return carry

    def transpose_weights(b, carry):
        for k in range(channels // 128):
            turned[128 * k : 128 * k + 128, :] = staged[b, :, 128 * k : 128 * k + 128].T
        for first, tiles in ((128 * step[0], step) for step in STEPS):
            width = 128 * len(tiles)
            for n, j in enumerate(tiles):
                for d in range(0, n_ens, 2):
                    low, high = 8 * (TILES * d + j), 8 * (TILES * (d + 1) + j)
                    hi, lo = split(jnp.concatenate([turned[low : low + 8, :], turned[high : high + 8, :]], axis=0))
                    to = pl.ds(pl.multiple_of(BASES * first + b * width + 128 * n + 8 * d, 16), 16)
                    m_hi[to, :] = hi
                    m_lo[to, :] = lo
        return carry

    start_halo(0, members_ref, every)
    stencil_matrices(0, stencils_ref, w_hi, w_lo, spaced, by_row)

    truth = padded(analysis_ref[...].reshape(cells, per), cells, 128)
    main, tail = truth[:128].T, padded(truth[128:], 128, 128).T
    for j in range(TILES):
        a_body[8 + 8 * j : 16 + 8 * j, :] = main[8 * j : 8 * j + 8]
        if j < 4:
            a_body[0:8, 32 * j : 32 * j + 32] = tail[8 * j : 8 * j + 8, 0:32]
        else:
            for c in range(8):
                a_rest[c // 4 : c // 4 + 1, 32 * (c % 4) : 32 * (c % 4) + 32] = tail[8 * j + c : 8 * j + c + 1, 0:32]

    lax.fori_loop(0, BASES, load_weights, 0)
    extend(0, members_ref, every)
    stencil(every)

    def body_copy(phase, step, src, dst, other, slot):
        first, count = STEP_ROWS[step]
        rows = pl.ds(first, count)
        return pltpu.make_async_remote_copy(
            src.at[other, rows], dst.at[slot, rows], a2a_send.at[phase, step, other], a2a_recv.at[phase, step, slot],
            device_id={"ens": other}, device_id_type=MESH,
        )

    def rest_copy(phase, src, dst, other, slot):
        return pltpu.make_async_remote_copy(
            src.at[other], dst.at[slot], a2a_send.at[phase, 3, other], a2a_recv.at[phase, 3, slot],
            device_id={"ens": other}, device_id_type=MESH,
        )

    def peers(action):
        def one(k, carry):
            action(lax.rem(ens + k, n_ens))
            return carry

        lax.fori_loop(1, n_ens, one, 0)

    done = 0
    for cols in chunks():
        width = cols.stop - cols.start
        activation = jnp.tanh(mix(cols, every))
        act[:, cols] = activation
        forecast = members_ref[:, :, cols].reshape(cells, width) + activation
        for c in range(width // 128):
            part = forecast[:, 128 * c : 128 * c + 128]
            main, tail = part[:128].T, padded(part[128:], 128, 128).T
            for n in range(16):
                k = (cols.start // 128 + c) * 16 + n
                d, j = k // TILES, k % TILES
                send1[d, 8 + 8 * j : 16 + 8 * j, :] = main[8 * n : 8 * n + 8]
                if j < 4:
                    send1[d, 0:8, 32 * j : 32 * j + 32] = tail[8 * n : 8 * n + 8, 0:32]
                else:
                    tails[d, :, 0:32] = tail[8 * n : 8 * n + 8, 0:32]
        for d in range(done, cols.stop // per):
            pl.when(ens != d)(body_copy(0, 0, send1, recv1, d, ens).start)
        done = cols.stop // per
    spread_rest(tails, rest1)
    peers(lambda other: rest_copy(0, rest1, got1, other, ens).start())
    for step in (1, 2):
        peers(lambda other: body_copy(0, step, send1, recv1, other, ens).start())
    recv1[ens] = send1[ens]
    got1[ens] = rest1[ens]

    lax.fori_loop(0, BASES, transpose_weights, 0)
    for c in range(channels // 128):
        damp = act[:, 128 * c : 128 * c + 128]
        damp = 1.0 - damp * damp
        damp_main[128 * c : 128 * c + 128, :] = damp[:128].T
        damp_tail[128 * c : 128 * c + 128, :] = padded(damp[128:], 128, 128).T

    members_total = n_ens
    diagonal = members_total * float(np.sqrt(np.float32(SMOOTH)))
    pairs_scale = 2.0 * members_total * (members_total - 1)

    def score(read, truth, write):
        x = [read(m) - truth for m in range(n_ens)]
        slope = [None] * n_ens
        own, pair_abs = None, None
        for m in range(n_ens):
            for n in range(m + 1, n_ens):
                d = x[m] - x[n]
                s2 = d * d + SMOOTH
                r = lax.rsqrt(s2)
                sl = d * r
                ab = s2 * r
                pair_abs = ab if pair_abs is None else pair_abs + ab
                slope[m] = sl if slope[m] is None else slope[m] + sl
                slope[n] = -sl if slope[n] is None else slope[n] - sl
            s2 = x[m] * x[m] + SMOOTH
            r = lax.rsqrt(s2)
            own = s2 * r if own is None else own + s2 * r
            write(m, x[m] * r - slope[m] * (1.0 / (members_total - 1.0)))
        return own * (1.0 / members_total) - (2.0 * pair_abs + diagonal) * (1.0 / pairs_scale)

    def score_rows(t, carry):
        rows = pl.ds(pl.multiple_of(8 * t, 8), 8)

        def write(m, value):
            send2[m, rows, :] = value

        c_body[rows, :] = score(lambda m: recv1[m, rows, :], a_body[rows, :], write)
        return carry

    def score_rest():
        def write(m, value):
            rest2[m] = value

        c_rest[...] = score(lambda m: got1[m], a_rest[...], write)

    for step in range(3):
        peers(lambda other: body_copy(0, step, send1, recv1, other, other).wait_recv())
        first, count = STEP_ROWS[step]
        lax.fori_loop(first // 8, (first + count) // 8, score_rows, 0)
        peers(lambda other: body_copy(1, step, send2, recv2, other, ens).start())
        if step == 0:
            peers(lambda other: rest_copy(0, rest1, got1, other, other).wait_recv())
            score_rest()
            peers(lambda other: rest_copy(1, rest2, got2, other, ens).start())
            stencil_matrices(1, stencils_ref, w_hi, w_lo, spaced, by_row)
    recv2[ens] = send2[ens]
    got2[ens] = rest2[ens]

    mains = [c_body[8 + 8 * j : 16 + 8 * j, :] for j in range(TILES)]
    parts = [c_body[0:8, 32 * j : 32 * j + 32] for j in range(4)]
    parts += [c_rest[c // 4 : c // 4 + 1, 32 * (c % 4) : 32 * (c % 4) + 32] for c in range(8)]
    main = padded(jnp.concatenate(mains, axis=0), 128, 128).T
    tail = padded(jnp.concatenate(parts, axis=0), 128, 128).T
    crps_ref[0:16] = main[:, 0:per].reshape(16, COLS, per)
    crps_ref[16:20] = tail[0:32, 0:per].reshape(4, COLS, per)

    def tile_tail(d, j):
        return recv2[d, 0:8, 32 * j : 32 * j + 32] if j < 4 else tails[d, :, 0:32]

    def returned(step):
        peers(lambda other: body_copy(1, step, send2, recv2, other, other).wait_recv())
        if step == 0:
            peers(lambda other: rest_copy(1, rest2, got2, other, other).wait_recv())
            gather_rest(got2, tails)
        for j in STEPS[step]:
            mains, parts = [], []
            for d in range(n_ens):
                at = slice(8 * (TILES * d + j), 8 * (TILES * d + j) + 8)
                mains.append(recv2[d, 8 + 8 * j : 16 + 8 * j, :] * damp_main[at, :])
                parts.append(tile_tail(d, j) * damp_tail[at, 0:32])
            main = jnp.concatenate(mains, axis=0).T
            tail = padded(jnp.concatenate(parts, axis=0), 128, 128).T
            cols = slice(128 * j, 128 * j + 128)
            field[0:16, :, cols] = main.reshape(16, COLS, 128)
            field[16:20, :, cols] = tail[0:32].reshape(4, COLS, 128)
        cols = slice(128 * STEPS[step][0], 128 * STEPS[step][-1] + 128)
        fill_packs(field, cols)
        start_halo(1 + step, field, cols)

    def adjoint(step):
        inputs = slice(128 * STEPS[step][0], 128 * STEPS[step][-1] + 128)
        extend(1 + step, field, inputs)
        stencil(inputs)
        for cols in chunks():
            more = mix(cols, inputs).reshape(ROWS, COLS, cols.stop - cols.start)
            grad_ref[:, :, cols] = more if step == 0 else grad_ref[:, :, cols] + more

    returned(0)
    returned(1)
    adjoint(0)
    returned(2)
    adjoint(1)
    for c in range(channels // 128):
        mains, parts = [], []
        for n in range(16):
            k = 16 * c + n
            d, j = k // TILES, k % TILES
            mains.append(recv2[d, 8 + 8 * j : 16 + 8 * j, :])
            parts.append(tile_tail(d, j))
        main = jnp.concatenate(mains, axis=0).T
        tail = padded(jnp.concatenate(parts, axis=0), 128, 128).T
        cols = slice(128 * c, 128 * c + 128)
        grad_ref[0:16, :, cols] = grad_ref[0:16, :, cols] + main.reshape(16, COLS, 128)
        grad_ref[16:20, :, cols] = grad_ref[16:20, :, cols] + tail[0:32].reshape(4, COLS, 128)
    adjoint(2)

    for phase, body, rest, there, got in ((0, send1, rest1, recv1, got1), (1, send2, rest2, recv2, got2)):
        for step in range(3):
            peers(lambda other: body_copy(phase, step, body, there, other, ens).wait_send())
        peers(lambda other: rest_copy(phase, rest, got, other, ens).wait_send())


def local(members, analysis, stencils, mixing):
    channels = members.shape[3]
    n_ens = lax.axis_size("ens")
    per = channels // n_ens
    depth = BASES * channels
    cells = ROWS * COLS
    vmem = pl.BlockSpec(memory_space=pltpu.VMEM)
    body = pltpu.VMEM((n_ens, BODY, 128), f32)
    rest = pltpu.VMEM((n_ens, 2, 128), f32)
    grad, crps = pl.pallas_call(
        step_kernel,
        out_shape=[
            jax.ShapeDtypeStruct((ROWS, COLS, channels), f32),
            jax.ShapeDtypeStruct((ROWS, COLS, per), f32),
        ],
        in_specs=[vmem] * 3 + [pl.BlockSpec(memory_space=pl.ANY)],
        out_specs=[vmem, vmem],
        scratch_shapes=[
            pltpu.VMEM((WINDOWS, 16 * BASES, 128), bf16),
            pltpu.VMEM((WINDOWS, 16 * BASES, 128), bf16),
            pltpu.VMEM((128, 128), f32),
            pltpu.VMEM((128, 128), f32),
            pltpu.VMEM((BASES, channels, channels), f32),
            pltpu.VMEM((channels, channels), f32),
            pltpu.VMEM((depth, channels), bf16),
            pltpu.VMEM((depth, channels), bf16),
            pltpu.VMEM((16 * EXT, channels), bf16),
            pltpu.VMEM((16 * EXT, channels), bf16),
            pltpu.VMEM((cells, depth), bf16),
            pltpu.VMEM((cells, depth), bf16),
            pltpu.VMEM((ROWS, COLS, channels), f32),
            pltpu.VMEM((cells, channels), f32),
            pltpu.VMEM((channels, 128), f32),
            pltpu.VMEM((channels, 128), f32),
            pltpu.VMEM((64, channels), f32),
            pltpu.VMEM((64, channels), f32),
            pltpu.VMEM((2, 2, 64, channels), f32),
            pltpu.VMEM((2, 2, MARGIN, COLS, channels), f32),
            pltpu.VMEM((2, 4, 16, channels), f32),
            pltpu.VMEM((BODY, 128), f32),
            pltpu.VMEM((2, 128), f32),
            pltpu.VMEM((BODY, 128), f32),
            pltpu.VMEM((2, 128), f32),
            pltpu.VMEM((n_ens, 8, 128), f32),
            body, rest, body, rest,
            body, rest, body, rest,
            pltpu.SemaphoreType.DMA((BASES,)),
            pltpu.SemaphoreType.DMA((4, 8)),
            pltpu.SemaphoreType.DMA((4, 8)),
            pltpu.SemaphoreType.DMA((2, 4, n_ens)),
            pltpu.SemaphoreType.DMA((2, 4, n_ens)),
        ],
        compiler_params=pltpu.CompilerParams(
            collective_id=0, has_side_effects=True, vmem_limit_bytes=56 * 1024 * 1024
        ),
        name="ensemble_step",
    )(members[0], analysis, stencils, mixing)
    return grad[None], crps


def solution(mesh):
    in_specs = (P("ens", "lat", "lon", None), P("lat", "lon", "ens"), P(), P())
    out_specs = (P("ens", "lat", "lon", None), P("lat", "lon", "ens"))
    return jax.shard_map(local, mesh=mesh, in_specs=in_specs, out_specs=out_specs, check_vma=False)
```

time: 69.8 us -> 63.7 us (0.913)
  the two profiles are of different devices: /device:TPU:5 before, /device:TPU:1 now
where the time goes in v3:
time: 63.7 us; the launch traced here: 63.5 us
  Pallas kernels  59.5 us (93%)
  local copies, waits for them, and re-layouts  3.31 us (5%)
  between operations  0.64 us (1%)
    pallas_call x1, Pallas kernels, local(): pl.pallas_call(step_kernel, out_shape=[jax.ShapeDtypeStruct((ROWS, COLS,...  59.5 us
    unnamed x2, local copies, waits for them, and re-layouts  3.31 us

profile of v3, /device:TPU:1, one launch (start us, length us, event | category | flops | bytes accessed | tf_op | source)
XLA Modules:
  0.0 63.5 jit_solution(9553834739818014863)
XLA Ops:
  0.6 59.5 %ensemble_step.1 = (f32[20,8,640]{2,1,0:T(8,128)}, f32[20,8,40]{2,1,0:T(8,128)}) custom-call(f32[20,8,640]{2,1,0:T(8,128)} %bitcast.3, f32[20,8,40]{2,1,0:T(8,128)} %analysis_ref.1, f32[7,7,7,80]{3,2,1,0:T(8,128)} %stencils_ref.1, f32[7,640,640]{2,1,0:T(8,128)} %mixing_ref.1), custom_call_target="tpu_custom_call" | custom-call | tf_op jit(solution)/shard_map/ensemble_step/pallas_call | solution.py:472
  60.2 1.8 %copy.8 = f32[1,20,8,640]{3,2,1,0:T(8,128)} copy(f32[1,20,8,640]{3,2,1,0:T(8,128)} %bitcast.2) | data formatting | bytes 819200
  62.0 1.5 %copy.9 = f32[20,8,40]{2,1,0:T(8,128)} copy(f32[20,8,40]{2,1,0:T(8,128)} %get-tuple-element.9) | data formatting | bytes 51200

commit v4 on v3

--- a/solution.py
+++ b/solution.py
@@ -92,8 +92,9 @@
 
 
 def step_kernel(
-    members_ref, analysis_ref, stencils_ref, mixing_ref,
+    members_hbm, analysis_hbm, stencils_hbm, mixing_ref,
     grad_ref, crps_ref,
+    members_ref, analysis_ref, stencils_ref, in_sem,
     w_hi, w_lo, spaced, by_row, staged, turned, m_hi, m_lo, e_hi, e_lo, s_hi, s_lo,
     field, act, damp_main, damp_tail, pack_r, pack_l, side, updown, corner,
     a_body, a_rest, c_body, c_rest, tails, send1, rest1, recv1, got1, send2, rest2, recv2, got2,
@@ -105,12 +106,28 @@
     ens, lat, lon = lax.axis_index("ens"), lax.axis_index("lat"), lax.axis_index("lon")
     right, left = lax.rem(lon + 1, n_lon), lax.rem(lon + n_lon - 1, n_lon)
     has_up, has_down = lat > 0, lat < n_lat - 1
-    channels = members_ref.shape[2]
+    channels = members_hbm.shape[2]
     cells = ROWS * COLS
     per = 8 * TILES
 
-    for b in range(BASES):
-        pltpu.make_async_copy(mixing_ref.at[b], staged.at[b], mix_sem.at[b]).start()
+    def chunks():
+        return [slice(c, min(c + 256, channels)) for c in range(0, channels, 256)]
+
+    loads = [
+        pltpu.make_async_copy(src, dst, in_sem.at[k])
+        for k, (src, dst) in enumerate(
+            ((members_hbm, members_ref), (stencils_hbm, stencils_ref), (analysis_hbm, analysis_ref))
+        )
+    ]
+    for load in loads:
+        load.start()
+
+    def weights_copy(n, cols):
+        rows = pl.ds(cols.start, cols.stop - cols.start)
+        return pltpu.make_async_copy(mixing_ref.at[:, rows], staged.at[:, rows], mix_sem.at[n])
+
+    for n, cols in enumerate(chunks()):
+        weights_copy(n, cols).start()
 
     barrier = pltpu.get_barrier_semaphore()
 
@@ -136,11 +153,13 @@
     every = slice(0, channels)
     pack_r[56:64, :] = jnp.zeros((8, channels), f32)
     pack_l[56:64, :] = jnp.zeros((8, channels), f32)
+    for load in loads:
+        load.wait()
     fill_packs(members_ref, every)
     pl.semaphore_wait(barrier, n_ens + 1 + 3 * has_up.astype(jnp.int32) + 3 * has_down.astype(jnp.int32))
 
     def halo_copies(phase, src, cols):
-        back = min(phase, 1)
+        back = phase // 3
         lanes = pl.ds(cols.start, cols.stop - cols.start)
 
         def remote(k, a, b, to):
@@ -195,9 +214,9 @@
 
     def extend(phase, src, cols):
         copies = halo_copies(phase, src, cols)
-        back = min(phase, 1)
+        back = phase // 3
         for k in (0, 1):
-            copies[k][2].wait()
+            copies[k][2].wait_recv()
         for r in range(ROWS):
             at = slice(3 * r, 3 * r + 3)
             put_row(r + MARGIN, src[r, :, cols], side[back, 1, at, cols], side[back, 0, at, cols], cols)
@@ -220,8 +239,13 @@
             def _():
                 for ref in (e_hi, e_lo):
                     ref[16 * first : 16 * first + 48, cols] = jnp.zeros((48, cols.stop - cols.start), bf16)
-        for k in range(2, 8):
-            pl.when(copies[k][0])(copies[k][2].wait_send)
+
+    def halo_sent(phase, src, cols):
+        for sends, _, copy in halo_copies(phase, src, cols):
+            if sends is None:
+                copy.wait_send()
+            else:
+                pl.when(sends)(copy.wait_send)
 
     def stencil(cols):
         width = cols.stop - cols.start
@@ -243,20 +267,27 @@
 
     def mix(cols, inputs):
         k = slice(BASES * inputs.start, BASES * inputs.stop)
-        weights = m_hi[k, cols]
-        return mm(s_hi[:, k], weights) + mm(s_lo[:, k], weights) + mm(s_hi[:, k], m_lo[k, cols])
-
-    def chunks():
-        return [slice(c, min(c + 256, channels)) for c in range(0, channels, 256)]
-
-    def load_weights(b, carry):
-        pltpu.make_async_copy(mixing_ref.at[b], staged.at[b], mix_sem.at[b]).wait()
-        for k in range(channels // 128):
-            hi, lo = split(staged[b, 128 * k : 128 * k + 128, :])
-            to = pl.ds(pl.multiple_of(b * channels + 128 * k, 128), 128)
-            m_hi[to, :] = hi
-            m_lo[to, :] = lo
-        return carry
+        weights, more = m_hi[k, cols], m_lo[k, cols]
+        width = cols.stop - cols.start
+        if width == 128:
+            both = mm(s_hi[:, k], jnp.concatenate([weights, more], axis=1))
+            return both[:, :128] + both[:, 128:] + mm(s_lo[:, k], weights)
+        return mm(s_hi[:, k], weights) + mm(s_lo[:, k], weights) + mm(s_hi[:, k], more)
+
+    def load_weights(n, cols):
+        weights_copy(n, cols).wait()
+        width = cols.stop - cols.start
+
+        def one_basis(b, carry):
+            for k in range(width // 128):
+                at = cols.start + 128 * k
+                hi, lo = split(staged[b, at : at + 128, :])
+                to = pl.ds(pl.multiple_of(BASES * cols.start + b * width + 128 * k, 128), 128)
+                m_hi[to, :] = hi
+                m_lo[to, :] = lo
+            return carry
+
+        lax.fori_loop(0, BASES, one_basis, 0)
 
     def transpose_weights(b, carry):
         for k in range(channels // 128):
@@ -272,22 +303,14 @@
                     m_lo[to, :] = lo
         return carry
 
-    start_halo(0, members_ref, every)
+    for n, cols in enumerate(chunks()):
+        start_halo(n, members_ref, cols)
     stencil_matrices(0, stencils_ref, w_hi, w_lo, spaced, by_row)
 
-    truth = padded(analysis_ref[...].reshape(cells, per), cells, 128)
-    main, tail = truth[:128].T, padded(truth[128:], 128, 128).T
-    for j in range(TILES):
-        a_body[8 + 8 * j : 16 + 8 * j, :] = main[8 * j : 8 * j + 8]
-        if j < 4:
-            a_body[0:8, 32 * j : 32 * j + 32] = tail[8 * j : 8 * j + 8, 0:32]
-        else:
-            for c in range(8):
-                a_rest[c // 4 : c // 4 + 1, 32 * (c % 4) : 32 * (c % 4) + 32] = tail[8 * j + c : 8 * j + c + 1, 0:32]
-
-    lax.fori_loop(0, BASES, load_weights, 0)
-    extend(0, members_ref, every)
-    stencil(every)
+    for n, inputs in enumerate(chunks()):
+        load_weights(n, inputs)
+        extend(n, members_ref, inputs)
+        stencil(inputs)
 
     def body_copy(phase, step, src, dst, other, slot):
         first, count = STEP_ROWS[step]
@@ -337,6 +360,19 @@
     recv1[ens] = send1[ens]
     got1[ens] = rest1[ens]
 
+    for n, cols in enumerate(chunks()):
+        halo_sent(n, members_ref, cols)
+
+    truth = padded(analysis_ref[...].reshape(cells, per), cells, 128)
+    main, tail = truth[:128].T, padded(truth[128:], 128, 128).T
+    for j in range(TILES):
+        a_body[8 + 8 * j : 16 + 8 * j, :] = main[8 * j : 8 * j + 8]
+        if j < 4:
+            a_body[0:8, 32 * j : 32 * j + 32] = tail[8 * j : 8 * j + 8, 0:32]
+        else:
+            for c in range(8):
+                a_rest[c // 4 : c // 4 + 1, 32 * (c % 4) : 32 * (c % 4) + 32] = tail[8 * j + c : 8 * j + c + 1, 0:32]
+
     lax.fori_loop(0, BASES, transpose_weights, 0)
     for c in range(channels // 128):
         damp = act[:, 128 * c : 128 * c + 128]
@@ -392,9 +428,9 @@
             peers(lambda other: rest_copy(0, rest1, got1, other, other).wait_recv())
             score_rest()
             peers(lambda other: rest_copy(1, rest2, got2, other, ens).start())
-            stencil_matrices(1, stencils_ref, w_hi, w_lo, spaced, by_row)
     recv2[ens] = send2[ens]
     got2[ens] = rest2[ens]
+    stencil_matrices(1, stencils_ref, w_hi, w_lo, spaced, by_row)
 
     mains = [c_body[8 + 8 * j : 16 + 8 * j, :] for j in range(TILES)]
     parts = [c_body[0:8, 32 * j : 32 * j + 32] for j in range(4)]
@@ -425,20 +461,19 @@
             field[16:20, :, cols] = tail[0:32].reshape(4, COLS, 128)
         cols = slice(128 * STEPS[step][0], 128 * STEPS[step][-1] + 128)
         fill_packs(field, cols)
-        start_halo(1 + step, field, cols)
+        start_halo(3 + step, field, cols)
 
     def adjoint(step):
         inputs = slice(128 * STEPS[step][0], 128 * STEPS[step][-1] + 128)
-        extend(1 + step, field, inputs)
+        extend(3 + step, field, inputs)
         stencil(inputs)
         for cols in chunks():
             more = mix(cols, inputs).reshape(ROWS, COLS, cols.stop - cols.start)
             grad_ref[:, :, cols] = more if step == 0 else grad_ref[:, :, cols] + more
 
-    returned(0)
-    returned(1)
+    for step in range(3):
+        returned(step)
     adjoint(0)
-    returned(2)
     adjoint(1)
     for c in range(channels // 128):
         mains, parts = [], []
@@ -453,11 +488,17 @@
         grad_ref[0:16, :, cols] = grad_ref[0:16, :, cols] + main.reshape(16, COLS, 128)
         grad_ref[16:20, :, cols] = grad_ref[16:20, :, cols] + tail[0:32].reshape(4, COLS, 128)
     adjoint(2)
-
+    for step, cols in enumerate(chunks()):
+        halo_sent(3 + step, field, cols)
     for phase, body, rest, there, got in ((0, send1, rest1, recv1, got1), (1, send2, rest2, recv2, got2)):
         for step in range(3):
             peers(lambda other: body_copy(phase, step, body, there, other, ens).wait_send())
         peers(lambda other: rest_copy(phase, rest, got, other, ens).wait_send())
+
+
+def keep(grad_ref, crps_ref, grad_out, crps_out):
+    grad_out[...] = grad_ref[...]
+    crps_out[...] = crps_ref[...]
 
 
 def local(members, analysis, stencils, mixing):
@@ -475,9 +516,13 @@
             jax.ShapeDtypeStruct((ROWS, COLS, channels), f32),
             jax.ShapeDtypeStruct((ROWS, COLS, per), f32),
         ],
-        in_specs=[vmem] * 3 + [pl.BlockSpec(memory_space=pl.ANY)],
+        in_specs=[pl.BlockSpec(memory_space=pl.ANY)] * 4,
         out_specs=[vmem, vmem],
         scratch_shapes=[
+            pltpu.VMEM(members.shape[1:], f32),
+            pltpu.VMEM(analysis.shape, f32),
+            pltpu.VMEM(stencils.shape, f32),
+            pltpu.SemaphoreType.DMA((3,)),
             pltpu.VMEM((WINDOWS, 16 * BASES, 128), bf16),
             pltpu.VMEM((WINDOWS, 16 * BASES, 128), bf16),
             pltpu.VMEM((128, 128), f32),
@@ -506,9 +551,9 @@
             pltpu.VMEM((n_ens, 8, 128), f32),
             body, rest, body, rest,
             body, rest, body, rest,
-            pltpu.SemaphoreType.DMA((BASES,)),
-            pltpu.SemaphoreType.DMA((4, 8)),
-            pltpu.SemaphoreType.DMA((4, 8)),
+            pltpu.SemaphoreType.DMA((3,)),
+            pltpu.SemaphoreType.DMA((6, 8)),
+            pltpu.SemaphoreType.DMA((6, 8)),
             pltpu.SemaphoreType.DMA((2, 4, n_ens)),
             pltpu.SemaphoreType.DMA((2, 4, n_ens)),
         ],
@@ -517,6 +562,13 @@
         ),
         name="ensemble_step",
     )(members[0], analysis, stencils, mixing)
+    grad, crps = pl.pallas_call(
+        keep,
+        out_shape=[jax.ShapeDtypeStruct(grad.shape, f32), jax.ShapeDtypeStruct(crps.shape, f32)],
+        in_specs=[vmem] * 2,
+        out_specs=[vmem] * 2,
+        name="results",
+    )(grad, crps)
     return grad[None], crps
 
 

time: 63.7 us -> 60 us (0.942)
  local copies, waits for them, and re-layouts: 3.31 us -> 0 us
    unnamed x2 -> x0, local copies, waits for them, and re-layouts: 3.31 us -> none
    pallas_call x1, Pallas kernels: 59.5 us -> 57.4 us  [local(): pl.pallas_call(step_kernel, out_shape=[jax.ShapeDtypeStruct((ROWS, COLS,...]
    pallas_call x0 -> x1, Pallas kernels: none -> 1.81 us  [local(): pl.pallas_call(keep, out_shape=[jax.ShapeDtypeStruct(grad.shape, f32), ja...]
where the time goes in v4:
time: 60 us; the launch traced here: 59.9 us
  Pallas kernels  59.2 us (99%)
  between operations  0.64 us (1%)
    pallas_call x1, Pallas kernels, local(): pl.pallas_call(step_kernel, out_shape=[jax.ShapeDtypeStruct((ROWS, COLS,...  57.4 us
    pallas_call x1, Pallas kernels, local(): pl.pallas_call(keep, out_shape=[jax.ShapeDtypeStruct(grad.shape, f32), ja...  1.81 us

profile of v4, /device:TPU:1, one launch (start us, length us, event | category | flops | bytes accessed | tf_op | source)
XLA Modules:
  0.0 59.9 jit_solution(216049004711032659)
XLA Ops:
  0.6 57.4 %ensemble_step.1 = (f32[20,8,640]{2,1,0:T(8,128)}, f32[20,8,40]{2,1,0:T(8,128)}) custom-call(f32[20,8,640]{2,1,0:T(8,128)} %bitcast.2, f32[20,8,40]{2,1,0:T(8,128)} %analysis_hbm.1, f32[7,7,7,80]{3,2,1,0:T(8,128)} %stencils_hbm.1, f32[7,640,640]{2,1,0:T(8,128)} %mixing_ref.1), custom_call_target="tpu_custom_call" | custom-call | tf_op jit(solution)/shard_map/ensemble_step/pallas_call | solution.py:513
  58.0 1.8 %results.1 = (f32[20,8,640]{2,1,0:T(8,128)}, f32[20,8,40]{2,1,0:T(8,128)}) custom-call(f32[20,8,640]{2,1,0:T(8,128)} %get-tuple-element.6.grad_ref, f32[20,8,40]{2,1,0:T(8,128)} %get-tuple-element.7.crps_ref), custom_call_target="tpu_custom_call" | custom-call | tf_op jit(solution)/shard_map/results/pallas_call | solution.py:565

commit v5 on v4

--- a/solution.py
+++ b/solution.py
@@ -66,21 +66,22 @@
 
 
 TILES = 5
-BODY = 8 * (TILES + 1)
+LAST = 8 * (TILES + 1)
+PIECE = LAST + 2
+PARTS = ((0, 24), (24, PIECE - 24))
 STEPS = ((0, 1), (2, 3), (4,))
-STEP_ROWS = ((0, 24), (24, 16), (40, 8))
-
-
-def spread_rest(tails, rest):
+
+
+def spread_rest(tails, pieces):
     for c in range(8):
-        lanes = slice(32 * (c % 4), 32 * (c % 4) + 32)
-        rest[:, c // 4, lanes] = tails[:, c, 0:32]
-
-
-def gather_rest(rest, tails):
+        row = LAST + c // 4
+        pieces[:, row, 32 * (c % 4) : 32 * (c % 4) + 32] = tails[:, c, 0:32]
+
+
+def gather_rest(pieces, tails):
     for c in range(8):
-        lanes = slice(32 * (c % 4), 32 * (c % 4) + 32)
-        tails[:, c, 0:32] = rest[:, c // 4, lanes]
+        row = LAST + c // 4
+        tails[:, c, 0:32] = pieces[:, row, 32 * (c % 4) : 32 * (c % 4) + 32]
 
 
 def padded(x, rows, lanes):
@@ -97,7 +98,7 @@
     members_ref, analysis_ref, stencils_ref, in_sem,
     w_hi, w_lo, spaced, by_row, staged, turned, m_hi, m_lo, e_hi, e_lo, s_hi, s_lo,
     field, act, damp_main, damp_tail, pack_r, pack_l, side, updown, corner,
-    a_body, a_rest, c_body, c_rest, tails, send1, rest1, recv1, got1, send2, rest2, recv2, got2,
+    a_piece, c_piece, tails, send1, recv1, send2, recv2,
     mix_sem, halo_send, halo_recv, a2a_send, a2a_recv,
 ):
     n_ens = lax.axis_size("ens")
@@ -312,17 +313,11 @@
         extend(n, members_ref, inputs)
         stencil(inputs)
 
-    def body_copy(phase, step, src, dst, other, slot):
-        first, count = STEP_ROWS[step]
+    def exchange(phase, part, src, dst, other, slot):
+        first, count = PARTS[part]
         rows = pl.ds(first, count)
         return pltpu.make_async_remote_copy(
-            src.at[other, rows], dst.at[slot, rows], a2a_send.at[phase, step, other], a2a_recv.at[phase, step, slot],
-            device_id={"ens": other}, device_id_type=MESH,
-        )
-
-    def rest_copy(phase, src, dst, other, slot):
-        return pltpu.make_async_remote_copy(
-            src.at[other], dst.at[slot], a2a_send.at[phase, 3, other], a2a_recv.at[phase, 3, slot],
+            src.at[other, rows], dst.at[slot, rows], a2a_send.at[phase, part, other], a2a_recv.at[phase, part, slot],
             device_id={"ens": other}, device_id_type=MESH,
         )
 
@@ -333,7 +328,6 @@
 
         lax.fori_loop(1, n_ens, one, 0)
 
-    done = 0
     for cols in chunks():
         width = cols.stop - cols.start
         activation = jnp.tanh(mix(cols, every))
@@ -350,15 +344,10 @@
                     send1[d, 0:8, 32 * j : 32 * j + 32] = tail[8 * n : 8 * n + 8, 0:32]
                 else:
                     tails[d, :, 0:32] = tail[8 * n : 8 * n + 8, 0:32]
-        for d in range(done, cols.stop // per):
-            pl.when(ens != d)(body_copy(0, 0, send1, recv1, d, ens).start)
-        done = cols.stop // per
-    spread_rest(tails, rest1)
-    peers(lambda other: rest_copy(0, rest1, got1, other, ens).start())
-    for step in (1, 2):
-        peers(lambda other: body_copy(0, step, send1, recv1, other, ens).start())
+    peers(lambda other: exchange(0, 0, send1, recv1, other, ens).start())
+    spread_rest(tails, send1)
+    peers(lambda other: exchange(0, 1, send1, recv1, other, ens).start())
     recv1[ens] = send1[ens]
-    got1[ens] = rest1[ens]
 
     for n, cols in enumerate(chunks()):
         halo_sent(n, members_ref, cols)
@@ -366,12 +355,13 @@
     truth = padded(analysis_ref[...].reshape(cells, per), cells, 128)
     main, tail = truth[:128].T, padded(truth[128:], 128, 128).T
     for j in range(TILES):
-        a_body[8 + 8 * j : 16 + 8 * j, :] = main[8 * j : 8 * j + 8]
+        a_piece[8 + 8 * j : 16 + 8 * j, :] = main[8 * j : 8 * j + 8]
         if j < 4:
-            a_body[0:8, 32 * j : 32 * j + 32] = tail[8 * j : 8 * j + 8, 0:32]
+            a_piece[0:8, 32 * j : 32 * j + 32] = tail[8 * j : 8 * j + 8, 0:32]
         else:
             for c in range(8):
-                a_rest[c // 4 : c // 4 + 1, 32 * (c % 4) : 32 * (c % 4) + 32] = tail[8 * j + c : 8 * j + c + 1, 0:32]
+                row = LAST + c // 4
+                a_piece[row : row + 1, 32 * (c % 4) : 32 * (c % 4) + 32] = tail[8 * j + c : 8 * j + c + 1, 0:32]
 
     lax.fori_loop(0, BASES, transpose_weights, 0)
     for c in range(channels // 128):
@@ -410,31 +400,29 @@
         def write(m, value):
             send2[m, rows, :] = value
 
-        c_body[rows, :] = score(lambda m: recv1[m, rows, :], a_body[rows, :], write)
+        c_piece[rows, :] = score(lambda m: recv1[m, rows, :], a_piece[rows, :], write)
         return carry
 
-    def score_rest():
-        def write(m, value):
-            rest2[m] = value
-
-        c_rest[...] = score(lambda m: got1[m], a_rest[...], write)
-
-    for step in range(3):
-        peers(lambda other: body_copy(0, step, send1, recv1, other, other).wait_recv())
-        first, count = STEP_ROWS[step]
+    for part in range(2):
+        peers(lambda other: exchange(0, part, send1, recv1, other, other).wait_recv())
+        first, count = PARTS[part]
         lax.fori_loop(first // 8, (first + count) // 8, score_rows, 0)
-        peers(lambda other: body_copy(1, step, send2, recv2, other, ens).start())
-        if step == 0:
-            peers(lambda other: rest_copy(0, rest1, got1, other, other).wait_recv())
-            score_rest()
-            peers(lambda other: rest_copy(1, rest2, got2, other, ens).start())
+        if part == 1:
+            rows = slice(LAST, PIECE)
+
+            def write_last(m, value):
+                send2[m, rows, :] = value
+
+            c_piece[rows, :] = score(lambda m: recv1[m, rows, :], a_piece[rows, :], write_last)
+        peers(lambda other: exchange(1, part, send2, recv2, other, ens).start())
     recv2[ens] = send2[ens]
-    got2[ens] = rest2[ens]
     stencil_matrices(1, stencils_ref, w_hi, w_lo, spaced, by_row)
 
-    mains = [c_body[8 + 8 * j : 16 + 8 * j, :] for j in range(TILES)]
-    parts = [c_body[0:8, 32 * j : 32 * j + 32] for j in range(4)]
-    parts += [c_rest[c // 4 : c // 4 + 1, 32 * (c % 4) : 32 * (c % 4) + 32] for c in range(8)]
+    mains = [c_piece[8 + 8 * j : 16 + 8 * j, :] for j in range(TILES)]
+    parts = [c_piece[0:8, 32 * j : 32 * j + 32] for j in range(4)]
+    for c in range(8):
+        row = LAST + c // 4
+        parts.append(c_piece[row : row + 1, 32 * (c % 4) : 32 * (c % 4) + 32])
     main = padded(jnp.concatenate(mains, axis=0), 128, 128).T
     tail = padded(jnp.concatenate(parts, axis=0), 128, 128).T
     crps_ref[0:16] = main[:, 0:per].reshape(16, COLS, per)
@@ -444,10 +432,10 @@
         return recv2[d, 0:8, 32 * j : 32 * j + 32] if j < 4 else tails[d, :, 0:32]
 
     def returned(step):
-        peers(lambda other: body_copy(1, step, send2, recv2, other, other).wait_recv())
-        if step == 0:
-            peers(lambda other: rest_copy(1, rest2, got2, other, other).wait_recv())
-            gather_rest(got2, tails)
+        if step < 2:
+            peers(lambda other: exchange(1, step, send2, recv2, other, other).wait_recv())
+        if step == 1:
+            gather_rest(recv2, tails)
         for j in STEPS[step]:
             mains, parts = [], []
             for d in range(n_ens):
@@ -490,10 +478,9 @@
     adjoint(2)
     for step, cols in enumerate(chunks()):
         halo_sent(3 + step, field, cols)
-    for phase, body, rest, there, got in ((0, send1, rest1, recv1, got1), (1, send2, rest2, recv2, got2)):
-        for step in range(3):
-            peers(lambda other: body_copy(phase, step, body, there, other, ens).wait_send())
-        peers(lambda other: rest_copy(phase, rest, got, other, ens).wait_send())
+    for phase, src, dst in ((0, send1, recv1), (1, send2, recv2)):
+        for part in range(2):
+            peers(lambda other: exchange(phase, part, src, dst, other, ens).wait_send())
 
 
 def keep(grad_ref, crps_ref, grad_out, crps_out):
@@ -508,8 +495,7 @@
     depth = BASES * channels
     cells = ROWS * COLS
     vmem = pl.BlockSpec(memory_space=pltpu.VMEM)
-    body = pltpu.VMEM((n_ens, BODY, 128), f32)
-    rest = pltpu.VMEM((n_ens, 2, 128), f32)
+    pieces = pltpu.VMEM((n_ens, PIECE, 128), f32)
     grad, crps = pl.pallas_call(
         step_kernel,
         out_shape=[
@@ -544,18 +530,15 @@
             pltpu.VMEM((2, 2, 64, channels), f32),
             pltpu.VMEM((2, 2, MARGIN, COLS, channels), f32),
             pltpu.VMEM((2, 4, 16, channels), f32),
-            pltpu.VMEM((BODY, 128), f32),
-            pltpu.VMEM((2, 128), f32),
-            pltpu.VMEM((BODY, 128), f32),
-            pltpu.VMEM((2, 128), f32),
+            pltpu.VMEM((PIECE, 128), f32),
+            pltpu.VMEM((PIECE, 128), f32),
             pltpu.VMEM((n_ens, 8, 128), f32),
-            body, rest, body, rest,
-            body, rest, body, rest,
+            pieces, pieces, pieces, pieces,
             pltpu.SemaphoreType.DMA((3,)),
             pltpu.SemaphoreType.DMA((6, 8)),
             pltpu.SemaphoreType.DMA((6, 8)),
-            pltpu.SemaphoreType.DMA((2, 4, n_ens)),
-            pltpu.SemaphoreType.DMA((2, 4, n_ens)),
+            pltpu.SemaphoreType.DMA((2, 2, n_ens)),
+            pltpu.SemaphoreType.DMA((2, 2, n_ens)),
         ],
         compiler_params=pltpu.CompilerParams(
             collective_id=0, has_side_effects=True, vmem_limit_bytes=56 * 1024 * 1024

time: 60 us -> 56.9 us (0.948); the launches traced: 59.9 us -> 55.9 us
  Pallas kernels: 59.2 us -> 55.3 us
    pallas_call x1, Pallas kernels: 57.4 us -> 53.5 us  [local(): pl.pallas_call(step_kernel, out_shape=[jax.ShapeDtypeStruct((ROWS, COLS,...]
where the time goes in v5:
time: 56.9 us; the launch traced here: 55.9 us
  Pallas kernels  55.3 us (97%)
  between operations  0.64 us (1%)
    pallas_call x1, Pallas kernels, local(): pl.pallas_call(step_kernel, out_shape=[jax.ShapeDtypeStruct((ROWS, COLS,...  53.5 us
    pallas_call x1, Pallas kernels, local(): pl.pallas_call(keep, out_shape=[jax.ShapeDtypeStruct(grad.shape, f32), ja...  1.81 us

profile of v5, /device:TPU:1, one launch (start us, length us, event | category | flops | bytes accessed | tf_op | source)
XLA Modules:
  0.0 55.9 jit_solution(7718979577068410589)
XLA Ops:
  0.6 53.5 %ensemble_step.1 = (f32[20,8,640]{2,1,0:T(8,128)}, f32[20,8,40]{2,1,0:T(8,128)}) custom-call(f32[20,8,640]{2,1,0:T(8,128)} %bitcast.2, f32[20,8,40]{2,1,0:T(8,128)} %analysis_hbm.1, f32[7,7,7,80]{3,2,1,0:T(8,128)} %stencils_hbm.1, f32[7,640,640]{2,1,0:T(8,128)} %mixing_ref.1), custom_call_target="tpu_custom_call" | custom-call | tf_op jit(solution)/shard_map/ensemble_step/pallas_call | solution.py:499
  54.1 1.8 %results.1 = (f32[20,8,640]{2,1,0:T(8,128)}, f32[20,8,40]{2,1,0:T(8,128)}) custom-call(f32[20,8,640]{2,1,0:T(8,128)} %get-tuple-element.6.grad_ref, f32[20,8,40]{2,1,0:T(8,128)} %get-tuple-element.7.crps_ref), custom_call_target="tpu_custom_call" | custom-call | tf_op jit(solution)/shard_map/results/pallas_call | solution.py:548

commit v6 on v5

--- a/solution.py
+++ b/solution.py
@@ -97,7 +97,7 @@
     grad_ref, crps_ref,
     members_ref, analysis_ref, stencils_ref, in_sem,
     w_hi, w_lo, spaced, by_row, staged, turned, m_hi, m_lo, e_hi, e_lo, s_hi, s_lo,
-    field, act, damp_main, damp_tail, pack_r, pack_l, side, updown, corner,
+    field, act, damp_main, damp_tail, pack_r, pack_l, low_r, low_l, side, updown, above, below,
     a_piece, c_piece, tails, send1, recv1, send2, recv2,
     mix_sem, halo_send, halo_recv, a2a_send, a2a_recv,
 ):
@@ -150,10 +150,11 @@
         for r in range(ROWS):
             pack_r[3 * r : 3 * r + 3, cols] = src[r, COLS - MARGIN : COLS, cols]
             pack_l[3 * r : 3 * r + 3, cols] = src[r, 0:MARGIN, cols]
+            if r < MARGIN:
+                low_r[3 * r : 3 * r + 3, cols] = src[r, COLS - MARGIN : COLS, cols]
+                low_l[3 * r : 3 * r + 3, cols] = src[r, 0:MARGIN, cols]
 
     every = slice(0, channels)
-    pack_r[56:64, :] = jnp.zeros((8, channels), f32)
-    pack_l[56:64, :] = jnp.zeros((8, channels), f32)
     for load in loads:
         load.wait()
     fill_packs(members_ref, every)
@@ -169,8 +170,7 @@
             )
 
         up, down = lat - 1, lat + 1
-        low = pl.ds(0, 16)
-        high = pl.ds(48, 16)
+        high = pl.ds(48, 12)
         return [
             (None, None, remote(0, pack_r.at[:, lanes], side.at[back, 0, :, lanes], {"lon": right})),
             (None, None, remote(1, pack_l.at[:, lanes], side.at[back, 1, :, lanes], {"lon": left})),
@@ -184,19 +184,19 @@
             ),
             (
                 has_down, has_up,
-                remote(4, pack_r.at[high, lanes], corner.at[back, 0, :, lanes], {"lat": down, "lon": right}),
+                remote(4, pack_r.at[high, lanes], above.at[back, 0, :, lanes], {"lat": down, "lon": right}),
             ),
             (
                 has_down, has_up,
-                remote(5, pack_l.at[high, lanes], corner.at[back, 1, :, lanes], {"lat": down, "lon": left}),
+                remote(5, pack_l.at[high, lanes], above.at[back, 1, :, lanes], {"lat": down, "lon": left}),
             ),
             (
                 has_up, has_down,
-                remote(6, pack_r.at[low, lanes], corner.at[back, 2, :, lanes], {"lat": up, "lon": right}),
+                remote(6, low_r.at[:, lanes], below.at[back, 0, :, lanes], {"lat": up, "lon": right}),
             ),
             (
                 has_up, has_down,
-                remote(7, pack_l.at[low, lanes], corner.at[back, 3, :, lanes], {"lat": up, "lon": left}),
+                remote(7, low_l.at[:, lanes], below.at[back, 1, :, lanes], {"lat": up, "lon": left}),
             ),
         ]
 
@@ -221,9 +221,9 @@
         for r in range(ROWS):
             at = slice(3 * r, 3 * r + 3)
             put_row(r + MARGIN, src[r, :, cols], side[back, 1, at, cols], side[back, 0, at, cols], cols)
-        for there, which, corners, first, offset in (
-            (has_up, 0, (0, 1), 0, 3),
-            (has_down, 1, (2, 3), ROWS + MARGIN, 0),
+        for there, which, corner, first, offset in (
+            (has_up, 0, above, 0, 3),
+            (has_down, 1, below, ROWS + MARGIN, 0),
         ):
             @pl.when(there)
             def _():
@@ -233,7 +233,7 @@
                     at = slice(offset + 3 * r, offset + 3 * r + 3)
                     put_row(
                         first + r, updown[back, which, r, :, cols],
-                        corner[back, corners[1], at, cols], corner[back, corners[0], at, cols], cols,
+                        corner[back, 1, at, cols], corner[back, 0, at, cols], cols,
                     )
 
             @pl.when(jnp.logical_not(there))
@@ -326,7 +326,7 @@
             action(lax.rem(ens + k, n_ens))
             return carry
 
-        lax.fori_loop(1, n_ens, one, 0)
+        lax.fori_loop(1, n_ens, one, 0, unroll=True)
 
     for cols in chunks():
         width = cols.stop - cols.start
@@ -525,11 +525,14 @@
             pltpu.VMEM((cells, channels), f32),
             pltpu.VMEM((channels, 128), f32),
             pltpu.VMEM((channels, 128), f32),
-            pltpu.VMEM((64, channels), f32),
-            pltpu.VMEM((64, channels), f32),
-            pltpu.VMEM((2, 2, 64, channels), f32),
+            pltpu.VMEM((3 * ROWS, channels), f32),
+            pltpu.VMEM((3 * ROWS, channels), f32),
+            pltpu.VMEM((9, channels), f32),
+            pltpu.VMEM((9, channels), f32),
+            pltpu.VMEM((2, 2, 3 * ROWS, channels), f32),
             pltpu.VMEM((2, 2, MARGIN, COLS, channels), f32),
-            pltpu.VMEM((2, 4, 16, channels), f32),
+            pltpu.VMEM((2, 2, 12, channels), f32),
+            pltpu.VMEM((2, 2, 9, channels), f32),
             pltpu.VMEM((PIECE, 128), f32),
             pltpu.VMEM((PIECE, 128), f32),
             pltpu.VMEM((n_ens, 8, 128), f32),

time: 56.9 us -> 56.2 us (0.988)
  Pallas kernels: 55.3 us -> 54.7 us
where the time goes in v6:
time: 56.2 us; the launch traced here: 55.3 us
  Pallas kernels  54.7 us (97%)
  between operations  0.64 us (1%)
    pallas_call x1, Pallas kernels, local(): pl.pallas_call(step_kernel, out_shape=[jax.ShapeDtypeStruct((ROWS, COLS,...  52.9 us
    pallas_call x1, Pallas kernels, local(): pl.pallas_call(keep, out_shape=[jax.ShapeDtypeStruct(grad.shape, f32), ja...  1.81 us

profile of v6, /device:TPU:1, one launch (start us, length us, event | category | flops | bytes accessed | tf_op | source)
XLA Modules:
  0.0 55.3 jit_solution(11403275463331671545)
XLA Ops:
  0.6 52.9 %ensemble_step.1 = (f32[20,8,640]{2,1,0:T(8,128)}, f32[20,8,40]{2,1,0:T(8,128)}) custom-call(f32[20,8,640]{2,1,0:T(8,128)} %bitcast.2, f32[20,8,40]{2,1,0:T(8,128)} %analysis_hbm.1, f32[7,7,7,80]{3,2,1,0:T(8,128)} %stencils_hbm.1, f32[7,640,640]{2,1,0:T(8,128)} %mixing_ref.1), custom_call_target="tpu_custom_call" | custom-call | tf_op jit(solution)/shard_map/ensemble_step/pallas_call | solution.py:499
  53.5 1.8 %results.1 = (f32[20,8,640]{2,1,0:T(8,128)}, f32[20,8,40]{2,1,0:T(8,128)}) custom-call(f32[20,8,640]{2,1,0:T(8,128)} %get-tuple-element.6.grad_ref, f32[20,8,40]{2,1,0:T(8,128)} %get-tuple-element.7.crps_ref), custom_call_target="tpu_custom_call" | custom-call | tf_op jit(solution)/shard_map/results/pallas_call | solution.py:551

commit v7 on v6

--- a/solution.py
+++ b/solution.py
@@ -364,12 +364,6 @@
                 a_piece[row : row + 1, 32 * (c % 4) : 32 * (c % 4) + 32] = tail[8 * j + c : 8 * j + c + 1, 0:32]
 
     lax.fori_loop(0, BASES, transpose_weights, 0)
-    for c in range(channels // 128):
-        damp = act[:, 128 * c : 128 * c + 128]
-        damp = 1.0 - damp * damp
-        damp_main[128 * c : 128 * c + 128, :] = damp[:128].T
-        damp_tail[128 * c : 128 * c + 128, :] = padded(damp[128:], 128, 128).T
-
     members_total = n_ens
     diagonal = members_total * float(np.sqrt(np.float32(SMOOTH)))
     pairs_scale = 2.0 * members_total * (members_total - 1)
@@ -416,6 +410,11 @@
             c_piece[rows, :] = score(lambda m: recv1[m, rows, :], a_piece[rows, :], write_last)
         peers(lambda other: exchange(1, part, send2, recv2, other, ens).start())
     recv2[ens] = send2[ens]
+    for c in range(channels // 128):
+        damp = act[:, 128 * c : 128 * c + 128]
+        damp = 1.0 - damp * damp
+        damp_main[128 * c : 128 * c + 128, :] = damp[:128].T
+        damp_tail[128 * c : 128 * c + 128, :] = padded(damp[128:], 128, 128).T
     stencil_matrices(1, stencils_ref, w_hi, w_lo, spaced, by_row)
 
     mains = [c_piece[8 + 8 * j : 16 + 8 * j, :] for j in range(TILES)]

time: 56.2 us -> 56.2 us (level)
  no operation moved by 1% of the time
where the time goes in v7:
time: 56.2 us; the launch traced here: 55.3 us
  Pallas kernels  54.7 us (97%)
  between operations  0.64 us (1%)
    pallas_call x1, Pallas kernels, local(): pl.pallas_call(step_kernel, out_shape=[jax.ShapeDtypeStruct((ROWS, COLS,...  52.9 us
    pallas_call x1, Pallas kernels, local(): pl.pallas_call(keep, out_shape=[jax.ShapeDtypeStruct(grad.shape, f32), ja...  1.81 us

profile of v7, /device:TPU:1, one launch (start us, length us, event | category | flops | bytes accessed | tf_op | source)
XLA Modules:
  0.0 55.3 jit_solution(13209678141843196962)
XLA Ops:
  0.6 52.9 %ensemble_step.1 = (f32[20,8,640]{2,1,0:T(8,128)}, f32[20,8,40]{2,1,0:T(8,128)}) custom-call(f32[20,8,640]{2,1,0:T(8,128)} %bitcast.2, f32[20,8,40]{2,1,0:T(8,128)} %analysis_hbm.1, f32[7,7,7,80]{3,2,1,0:T(8,128)} %stencils_hbm.1, f32[7,640,640]{2,1,0:T(8,128)} %mixing_ref.1), custom_call_target="tpu_custom_call" | custom-call | tf_op jit(solution)/shard_map/ensemble_step/pallas_call | solution.py:498
  53.5 1.8 %results.1 = (f32[20,8,640]{2,1,0:T(8,128)}, f32[20,8,40]{2,1,0:T(8,128)}) custom-call(f32[20,8,640]{2,1,0:T(8,128)} %get-tuple-element.6.grad_ref, f32[20,8,40]{2,1,0:T(8,128)} %get-tuple-element.7.crps_ref), custom_call_target="tpu_custom_call" | custom-call | tf_op jit(solution)/shard_map/results/pallas_call | solution.py:550
